TPU v7x, 32 devices: a whole 2x2x4 slice. The times are simulated.
32 devices in a mesh: seq: 8 (over z, y), head: 4 (over x, core).
Axes of the slice: x: 2, y: 2, z: 4, core: 2. Of those that a mesh axis runs over, the one named last changes fastest.
Arguments:
- queries: bfloat16 [1280, 2560], P('seq', 'head'), may hold values from -48 to 48
- keys: bfloat16 [1280, 2560], P('seq', 'head'), may hold values from -9.625 to 9.625
- values: bfloat16 [1280, 2560], P('seq', 'head'), may hold values from -6 to 6
- out_weight: bfloat16 [2560, 5120], P('head'), may hold values from -0.125 to 0.125
Outputs:
- mixed: bfloat16 [1280, 5120], P('seq', 'head')
All inputs are finite; a program needn't handle non-finite values.
Results may differ from a plain program's by a relative error of at most 0.015.
Values may be sent and summed in bfloat16 or wider, within the bound.
No kernel may reach another device: no remote copies, remote signals or barrier semaphores. Data moves between devices by JAX's collectives and lax.ppermute only.
A program may use at most 192 MiB of HBM per device.

v0:
```python
import math

import jax
import jax.numpy as jnp
from jax import lax
from jax.sharding import PartitionSpec as P

HD = 128


def block_partial(query_rows, key_block, value_block, scale):
    scores = (
        jnp.einsum("rhd,bhd->hrb", query_rows, key_block, preferred_element_type=jnp.float32)
        * scale
    )
    block_max = jnp.max(scores, axis=-1)
    expo = jnp.exp(scores - block_max[..., None])
    block_total = jnp.sum(expo, axis=-1)
    weights = expo.astype(jnp.bfloat16)
    summed = jnp.einsum("hrb,bhd->rhd", weights, value_block, preferred_element_type=jnp.float32)
    partial_value = (summed / jnp.transpose(block_total)[..., None]).astype(jnp.bfloat16)
    block_log = jnp.transpose(block_max + jnp.log(block_total))
    return (partial_value, block_log)


def group_size(count):
    return max([divisor for divisor in range(1, 9) if count % divisor == 0])


def on_device(queries, keys, values, out_weight):
    rows = queries.shape[0]
    width = queries.shape[1]
    heads = width // HD
    scale = 1.0 / math.sqrt(HD)
    query_local = queries.reshape(rows, heads, HD)
    start_state = (
        jnp.full((rows, heads), -1e30, jnp.float32),
        jnp.zeros((rows, heads, HD), jnp.float32),
    )
    pieces = (
        lax.all_gather(keys, "seq", axis=0, tiled=True),
        lax.all_gather(values, "seq", axis=0, tiled=True),
    )
    count = pieces[0].shape[0] // rows
    group = group_size(count)
    key_groups = pieces[0].reshape(count // group, group, rows, heads, HD)
    value_groups = pieces[1].reshape(count // group, group, rows, heads, HD)

    def one_block(key_block, value_block):
        return block_partial(query_local, key_block, value_block, scale)

    def step_group(state, blocks_in):
        partial_value, block_log = jax.vmap(one_block)(blocks_in[0], blocks_in[1])
        run_log, accum = state
        highest = jnp.maximum(run_log, jnp.max(block_log, axis=0))
        new_log = highest + jnp.log(
            jnp.exp(run_log - highest) + jnp.sum(jnp.exp(block_log - highest), axis=0)
        )
        accum = accum * jnp.exp(run_log - new_log)[..., None]
        accum = accum + jnp.sum(partial_value * jnp.exp(block_log - new_log)[..., None], axis=0)
        return ((new_log, accum), None)

    final_state, unused = lax.scan(step_group, start_state, (key_groups, value_groups))
    attended = final_state[1]
    attended_rows = attended.astype(jnp.bfloat16).reshape(rows, width)
    term = jnp.dot(attended_rows, out_weight, preferred_element_type=jnp.float32)
    return lax.psum_scatter(term.astype(jnp.bfloat16), "head", scatter_dimension=1, tiled=True)


def solution(mesh):
    placed = (P("seq", "head"), P("seq", "head"), P("seq", "head"), P("head", None))
    return jax.shard_map(
        on_device, mesh=mesh, in_specs=placed, out_specs=P("seq", "head"), check_vma=False
    )
```

profile of v0, /device:TPU:0, one launch (start us, length us, event | category | flops | bytes accessed | tf_op | source)
XLA Modules:
  0.0 148.9 jit_solution(16688547008530719243)
XLA Ops:
  6.5 0.0 copy-start
  6.5 0.0 all-gather.3.cloned.1.call-start
  6.5 0.7 all-gather.3.cloned.1.call-update
  7.3 0.0 all-gather.5.cloned.1.call-start
  7.3 0.7 all-gather.5.cloned.1.call-update
  8.0 0.0 reduce-scatter.2.cloned.1.call-start
  8.1 49.0 %all-gather.3.cloned.1.call-done = bf16[1280,640]{1,0:T(8,128)(2,1)} async-done(((bf16[160,640]{1,0:T(8,128)(2,1)}), bf16[1280,640]{1,0:T(8,128)(2,1)}) %all-gather.3.cloned.1.call-update) | async-done | bytes 1638416 | tf_op jit(solution)/shard_map/all_gather | solution.py:41
  57.1 3.4 %squeeze.9 = bf16[8,160,5,128]{3,2,1,0:T(8,128)(2,1)S(1)} reshape(bf16[1280,640]{1,0:T(8,128)(2,1)} %all-gather.3.cloned.1.call-done) | data formatting | bytes 3276800 | tf_op jit(solution)/shard_map/while/body/jit(dynamic_index_in_dim)/squeeze | solution.py:63
  60.6 0.3 copy.19
  60.8 0.0 copy-done
  60.8 1.0 fusion.14
  61.9 0.9 multiply_reduce_fusion
  62.7 3.3 %fusion.1 = (bf16[8,5,160,160]{2,3,0,1:T(8,128)(2,1)}, f32[8,5,160]{2,0,1:T(8,128)S(1)}) fusion(f32[5,160,8,160]{1,3,2,0:T(8,128)S(1)} %bitcast.52, f32[8,5,160]{2,0,1:T(8,128)S(1)} %bitcast.56), kind=kLoop, calls=%fused_computation.4 | loop fusion | flops 4089600 | bytes 6195200 | tf_op jit(solution)/shard_map/while/body/eval_jaxpr/vmap()/convert_element_type | solution.py:19
  66.2 36.3 %all-gather.5.cloned.1.call-done = bf16[1280,640]{1,0:T(8,128)(2,1)} async-done(((bf16[160,640]{1,0:T(8,128)(2,1)}), bf16[1280,640]{1,0:T(8,128)(2,1)}) %all-gather.5.cloned.1.call-update) | async-done | bytes 1638416 | tf_op jit(solution)/shard_map/all_gather | solution.py:42
  102.5 0.0 slice-start
  102.5 4.8 %squeeze.10 = bf16[8,160,5,128]{3,2,1,0:T(8,128)(2,1)} reshape(bf16[1280,640]{1,0:T(8,128)(2,1)} %all-gather.5.cloned.1.call-done) | data formatting | bytes 3276800 | tf_op jit(solution)/shard_map/while/body/jit(dynamic_index_in_dim)/squeeze | solution.py:63
  107.3 0.0 slice-start.1
  107.3 5.4 %multiply_reduce_fusion.1 = f32[160,5,128]{2,0,1:T(8,128)S(1)} fusion(f32[8,160,5]{1,2,0:T(8,128)S(1)} %copy.23, f32[8,160,5]{1,2,0:T(8,128)S(1)} %copy.22, bf16[8,160,5,128]{3,2,1,0:T(8,128)(2,1)} %squeeze.10, bf16[8,5,160,160]{2,3,0,1:T(8,128)(2,1)} %get-tuple-element.17), kind=kOutput, calls=%fused_computation.10 | convolution fusion | flops 266137600 | bytes 4147200 | tf_op jit(solution)/shard_map/while/body/eval_jaxpr/vmap(hrb,bhd->rhd)/dot_general | solution.py:20
  112.7 0.0 slice-done
  112.7 0.0 slice-done.1
  112.8 2.7 %convolution_convert_fusion = bf16[160,5120]{1,0:T(8,128)(2,1)} fusion(bf16[640,5120]{1,0:T(8,128)(2,1)S(1)} %bitcast.54, f32[160,5,128]{2,0,1:T(8,128)S(1)} %multiply_reduce_fusion.1, f32[160,5]{0,1:T(8,128)S(1)} %get-tuple-element.15), kind=kOutput, calls=%fused_computation.3 | convolution fusion | flops 1049600000 | bytes 8604800 | tf_op jit(solution)/shard_map/dot_general | solution.py:66
  115.5 0.0 reduce-scatter.2.cloned.1.call-update
  115.5 26.9 %reduce-scatter.2.cloned.1.call-done = bf16[160,1280]{1,0:T(8,128)(2,1)} async-done(((bf16[160,5120]{1,0:T(8,128)(2,1)}), bf16[160,1280]{1,0:T(8,128)(2,1)}) %reduce-scatter.2.cloned.1.call-update) | async-done | bytes 409616 | tf_op jit(solution)/shard_map/reduce_scatter | solution.py:67
  (8 shorter events, 0.1 us)
Async XLA Ops:
  6.5 54.3 %copy-start = (bf16[160,640]{1,0:T(8,128)(2,1)S(1)}, bf16[160,640]{1,0:T(8,128)(2,1)}, u32[]{:S(2)}) copy-start(bf16[160,640]{1,0:T(8,128)(2,1)} %param.4) | copy-start | bytes 614404
  6.5 50.6 %all-gather.3.cloned.1.call-start = ((), (), s32[]{:S(2)}) async-start(), calls=%async_computation.1 | async-start | bytes 1843200 | tf_op jit(solution)/shard_map/all_gather | solution.py:41
  7.3 95.3 %all-gather.5.cloned.1.call-start = ((), (), s32[]{:S(2)}) async-start(), calls=%async_computation.2 | async-start | bytes 1843200 | tf_op jit(solution)/shard_map/all_gather | solution.py:42
  8.0 134.4 %reduce-scatter.2.cloned.1.call-start = ((), (), s32[]{:S(2)}) async-start(), calls=%async_computation.3 | async-start | bytes 2048000 | tf_op jit(solution)/shard_map/reduce_scatter | solution.py:67
  102.5 10.2 %slice-start = ((s8[6553600]{0:T(1024)(128)(4,1)}), s8[2359296]{0:T(1024)(128)(4,1)S(1)}, s32[]{:S(2)}) async-start(s8[6553600]{0:T(1024)(128)(4,1)} %bitcast.53), calls=%async_computation.4 | async-start | bytes 4718592
  107.3 5.4 %slice-start.1 = ((s8[6553600]{0:T(1024)(128)(4,1)}), s8[4194304]{0:T(1024)(128)(4,1)S(1)}, s32[]{:S(2)}) async-start(s8[6553600]{0:T(1024)(128)(4,1)} %bitcast.53), calls=%async_computation.5 | async-start | bytes 8388608
Sparse Core Ops, SparseCore 0:
  9.5 47.5 all-gather.2
  59.3 43.1 all-gather.4
  115.6 26.7 reduce-scatter.1
where the time goes:
time: 149 us
  waiting for transfers between devices  114 us (77%)
  between operations  13.2 us (9%)
  matrix products  9.13 us (6%)
  local copies, waits for them, and re-layouts  8.55 us (6%)
  other arithmetic  4.28 us (3%)
    all_gather x1, waiting for transfers between devices, on_device(): lax.all_gather(keys, 'seq', axis=0, tiled=True)  49 us
    all_gather x1, waiting for transfers between devices, on_device(): lax.all_gather(values, 'seq', axis=0, tiled=True)  36.3 us
    reduce_scatter x1, waiting for transfers between devices, on_device(): lax.psum_scatter(term.astype(jnp.bfloat16), 'head', scatter_dimension=1,...  26.9 us
    squeeze x3, local copies, waits for them, and re-layouts, on_device(): lax.scan(step_group, start_state, (key_groups, value_groups))  8.5 us
    dot_general x1, matrix products, block_partial(): jnp.einsum('hrb,bhd->rhd', weights, value_block, preferred_element_type=j...  5.4 us
    convert_element_type x1, other arithmetic, block_partial(): weights = expo.astype(jnp.bfloat16)  3.32 us
  transfers between devices with their start and end apart: 3, of which 3 were waited for; matrix products, arithmetic and copies ran while one was open for 6% of the time, Pallas kernels for 0%

commit v1 on v0

v1 whole, which is shorter than its diff:
```python
import functools
import math

import jax
import jax.numpy as jnp
from jax import lax
from jax.experimental import pallas as pl
from jax.experimental.pallas import tpu as pltpu
from jax.sharding import PartitionSpec as P


HD = 128
VM = pl.BlockSpec(memory_space=pltpu.VMEM)
GRANT = 8 * 2**20


def params():
    return pltpu.CompilerParams(vmem_limit_bytes=GRANT)


def flash_kernel(heads, blocks, first, last, *refs):
    q_ref = refs[0]
    k_refs = refs[1 : 1 + blocks]
    v_refs = refs[1 + blocks : 1 + 2 * blocks]
    rest = refs[1 + 2 * blocks :]
    rows = q_ref.shape[0]
    if not first:
        acc_in, top_in, total_in = rest[:3]
        rest = rest[3:]
    factor = math.log2(math.e) / math.sqrt(HD)
    for h in range(heads):
        cols = slice(h * HD, (h + 1) * HD)
        key = jnp.concatenate([ref[:, cols] for ref in k_refs], axis=0)
        value = jnp.concatenate([ref[:, cols] for ref in v_refs], axis=0)
        scores = factor * lax.dot_general(
            q_ref[:, cols], key, (((1,), (1,)), ((), ())), preferred_element_type=jnp.float32
        )
        top = jnp.max(scores, axis=1, keepdims=True)
        if not first:
            old_top = top_in[:, cols]
            wide_top = jnp.maximum(jnp.broadcast_to(top, (rows, HD)), old_top)
            top = wide_top[:, :1]
        else:
            wide_top = jnp.broadcast_to(top, (rows, HD))
        expo = jnp.exp2(scores - top)
        total = jnp.broadcast_to(jnp.sum(expo, axis=1, keepdims=True), (rows, HD))
        summed = jnp.dot(expo.astype(jnp.bfloat16), value, preferred_element_type=jnp.float32)
        if not first:
            shrink = jnp.exp2(old_top - wide_top)
            total = total + shrink * total_in[:, cols]
            summed = summed + shrink * acc_in[:, cols]
        if last:
            rest[0][:, cols] = (summed * jnp.exp2(-jnp.log2(total))).astype(jnp.bfloat16)
        else:
            rest[0][:, cols] = summed
            rest[1][:, cols] = wide_top
            rest[2][:, cols] = total


def flash(query, keys, values, state, last):
    rows, width = query.shape
    heads = width // HD
    blocks = len(keys)
    count = sum(k.shape[0] for k in keys)
    if last:
        out_shape = jax.ShapeDtypeStruct((rows, width), jnp.bfloat16)
        out_specs = VM
    else:
        out_shape = [jax.ShapeDtypeStruct((rows, width), jnp.float32)] * 3
        out_specs = [VM] * 3
    args = (query, *keys, *values, *state)
    return pl.pallas_call(
        functools.partial(flash_kernel, heads, blocks, not state, last),
        out_shape=out_shape,
        in_specs=[VM] * len(args),
        out_specs=out_specs,
        cost_estimate=pl.CostEstimate(
            flops=4 * rows * count * width,
            transcendentals=rows * count * heads,
            bytes_accessed=2 * rows * width * (1 + 2 * blocks) + 24 * rows * width,
        ),
        compiler_params=params(),
        name="flash",
    )(*args)


def weights_kernel(chips, columns, w_ref, mine_ref, other_ref, sems):
    place = lax.axis_index("head")
    copies = []
    for p in range(chips):
        target = lax.rem(place // 2 + p + 1, chips)
        for side, out in enumerate((mine_ref, other_ref)):
            core = place % 2 if side == 0 else 1 - place % 2
            start = pl.multiple_of((2 * target + core) * columns, HD)
            copy = pltpu.make_async_copy(
                w_ref.at[:, pl.ds(start, columns)],
                out.at[:, pl.ds(p * columns, columns)],
                sems.at[2 * p + side],
            )
            copy.start()
            copies.append(copy)
    for copy in copies:
        copy.wait()


def split_weights(weight, chips, columns):
    depth = weight.shape[0]
    half = jax.ShapeDtypeStruct((depth, chips * columns), weight.dtype)
    return pl.pallas_call(
        functools.partial(weights_kernel, chips, columns),
        out_shape=(half, half),
        in_specs=[pl.BlockSpec(memory_space=pl.ANY)],
        out_specs=(VM, VM),
        scratch_shapes=[pltpu.SemaphoreType.DMA((2 * chips,))],
        cost_estimate=pl.CostEstimate(
            flops=0, transcendentals=0, bytes_accessed=8 * depth * chips * columns
        ),
        compiler_params=pltpu.CompilerParams(vmem_limit_bytes=2 * GRANT),
        name="split_weights",
    )(weight)


def project_kernel(first, tile, a_ref, w_ref, *refs):
    out_ref = refs[-1]
    for start in range(0, out_ref.shape[1], tile):
        value = jnp.dot(
            a_ref[...],
            w_ref[:, first + start : first + start + tile],
            preferred_element_type=jnp.float32,
        )
        if len(refs) > 1:
            value = value + refs[0][:, start : start + tile]
        out_ref[:, start : start + tile] = value.astype(out_ref.dtype)


def project(rows_in, weight, first, columns, base, dtype):
    rows, depth = rows_in.shape
    tile = 256 if columns % 256 == 0 else HD
    args = (rows_in, weight) if base is None else (rows_in, weight, base)
    return pl.pallas_call(
        functools.partial(project_kernel, first, tile),
        out_shape=jax.ShapeDtypeStruct((rows, columns), dtype),
        in_specs=[VM] * len(args),
        out_specs=VM,
        cost_estimate=pl.CostEstimate(
            flops=2 * rows * depth * columns,
            transcendentals=0,
            bytes_accessed=2 * depth * columns + 4 * rows * columns,
        ),
        compiler_params=params(),
        name="project",
    )(*args)


def finish_kernel(arrived, *refs):
    total = refs[0][...]
    for ref in refs[1 : 1 + arrived]:
        total = total + ref[...].astype(jnp.float32)
    refs[-1][...] = total.astype(refs[-1].dtype)


def finish(mine, parts, index, pieces, output):
    rows, columns = mine.shape
    args = (mine, *parts)
    specs = [VM] * len(args)
    aliases = {}
    if output is not None:
        aliases = {len(args): 0}
        args += (output,)
        specs.append(pl.BlockSpec(memory_space=pl.ANY))
    return pl.pallas_call(
        functools.partial(finish_kernel, len(parts)),
        out_shape=jax.ShapeDtypeStruct((rows, columns * pieces), jnp.bfloat16),
        grid=(1,),
        in_specs=specs,
        out_specs=pl.BlockSpec((rows, columns), lambda i: (0, index)),
        input_output_aliases=aliases,
        cost_estimate=pl.CostEstimate(
            flops=rows * columns, transcendentals=0, bytes_accessed=8 * rows * columns
        ),
        compiler_params=params(),
        name="finish",
    )(*args)


def ring_pairs(n):
    order = list(range(0, n, 2)) + list(range(1, n, 2))[::-1]
    ahead = [(order[i], order[(i + 1) % n]) for i in range(n)]
    return ahead, [(b, a) for a, b in ahead]


def on_device(n_seq, n_head, queries, keys, values, out_weight):
    ahead, back = ring_pairs(n_seq)
    columns = out_weight.shape[1] // n_head
    chips = n_head // 2
    swap = [(i, i ^ 1) for i in range(n_head)]
    pieces = 2
    piece = columns // pieces
    steps = n_seq // 2

    w_mine, w_give = split_weights(out_weight, chips, columns)
    w_partner = lax.ppermute(w_give, "head", swap)
    state = flash(queries, [keys], [values], (), False)
    kf = kb = keys
    vf = vb = values
    for _ in range(1, steps):
        kf = lax.ppermute(kf, "seq", ahead)
        vb = lax.ppermute(vb, "seq", back)
        vf = lax.ppermute(vf, "seq", ahead)
        kb = lax.ppermute(kb, "seq", back)
        state = flash(queries, [kf, kb], [vf, vb], state, False)
    kf = lax.ppermute(kf, "seq", ahead)
    vb = lax.ppermute(vb, "seq", back)
    attended = flash(queries, [kf], [vb], state, True)
    partner = lax.ppermute(attended, "head", swap)

    arrived = [[] for _ in range(pieces)]
    for hop in range(1, chips):
        pairs = [(i, (i + 2 * hop) % n_head) for i in range(n_head)]
        for index in range(pieces):
            first = (hop - 1) * columns + index * piece
            part = project(attended, w_mine, first, piece, None, jnp.float32)
            part = project(partner, w_partner, first, piece, part, jnp.bfloat16)
            arrived[index].append(lax.ppermute(part, "head", pairs))
    output = None
    for index in range(pieces):
        first = (chips - 1) * columns + index * piece
        total = project(attended, w_mine, first, piece, None, jnp.float32)
        total = project(partner, w_partner, first, piece, total, jnp.float32)
        output = finish(total, arrived[index], index, pieces, output)
    return output


def solution(mesh):
    n_seq, n_head = mesh.shape["seq"], mesh.shape["head"]
    placed = (P("seq", "head"), P("seq", "head"), P("seq", "head"), P("head", None))
    return jax.shard_map(
        functools.partial(on_device, n_seq, n_head),
        mesh=mesh,
        in_specs=placed,
        out_specs=P("seq", "head"),
        check_vma=False,
    )
```

time: 149 us -> 56.4 us (0.38)
  waiting for transfers between devices: 114 us -> 21.8 us
  starting transfers between devices: 0.08 us -> 17.8 us
  Pallas kernels: 0 us -> 13.6 us
  between operations: 13.2 us -> 0.15 us
  matrix products: 9.13 us -> 0 us
  local copies, waits for them, and re-layouts: 8.55 us -> 2.87 us
  other arithmetic: 4.28 us -> 0 us
    all_gather x2 -> x0, waiting for transfers between devices: 85.3 us -> none  [the longest x1 49 us: on_device(): lax.all_gather(keys, 'seq', axis=0, tiled=True)]
    reduce_scatter x1 -> x0, waiting for transfers between devices: 26.9 us -> none  [on_device(): lax.psum_scatter(term.astype(jnp.bfloat16), 'head', scatter_dimension=1,...]
    ppermute x0 -> x18, waiting for transfers between devices: none -> 21.8 us  [the longest x3 8.75 us: on_device(): kb = lax.ppermute(kb, 'seq', back)]
    ppermute x0 -> x18, starting transfers between devices: none -> 17.8 us  [the longest x4 8.91 us: on_device(): kf = lax.ppermute(kf, 'seq', ahead)]
    pallas_call x0 -> x16, Pallas kernels: none -> 13.6 us  [the longest x5 7.94 us: flash(): pl.pallas_call(functools.partial(flash_kernel, heads, blocks, not state,...]
    squeeze x3 -> x0, local copies, waits for them, and re-layouts: 8.5 us -> none  [on_device(): lax.scan(step_group, start_state, (key_groups, value_groups))]
    dot_general x2 -> x0, matrix products: 8.1 us -> none  [the longest x1 5.4 us: block_partial(): jnp.einsum('hrb,bhd->rhd', weights, value_block, preferred_element_type=j...]
    convert_element_type x1 -> x0, other arithmetic: 3.32 us -> none  [block_partial(): weights = expo.astype(jnp.bfloat16)]
  transfers between devices with their start and end apart: 3 -> 18, of which waited for: 3 -> 9; matrix products, arithmetic and copies ran while one was open for 6% -> 0% of each run, Pallas kernels for 0% -> 21%
where the time goes in v1:
time: 56.4 us; the launch traced here: 56.3 us
  waiting for transfers between devices  21.8 us (39%)
  starting transfers between devices  17.8 us (32%)
  Pallas kernels  13.6 us (24%)
  local copies, waits for them, and re-layouts  2.87 us (5%)
    ppermute x4, starting transfers between devices, on_device(): kf = lax.ppermute(kf, 'seq', ahead)  8.91 us
    ppermute x3, waiting for transfers between devices, on_device(): kb = lax.ppermute(kb, 'seq', back)  8.75 us
    pallas_call x5, Pallas kernels, flash(): pl.pallas_call(functools.partial(flash_kernel, heads, blocks, not state,...  7.94 us
    ppermute x2, waiting for transfers between devices, on_device(): arrived[index].append(lax.ppermute(part, 'head', pairs))  6.59 us
    ppermute x4, waiting for transfers between devices, on_device(): kf = lax.ppermute(kf, 'seq', ahead)  4.82 us
    ppermute x3, starting transfers between devices, on_device(): vf = lax.ppermute(vf, 'seq', ahead)  4.11 us
    pallas_call x8, Pallas kernels, project(): pl.pallas_call(functools.partial(project_kernel, first, tile), out_shape=...  3.32 us
    unnamed x8, local copies, waits for them, and re-layouts  2.87 us
  transfers between devices with their start and end apart: 18, of which 9 were waited for; matrix products, arithmetic and copies ran while one was open for 0% of the time, Pallas kernels for 21%

profile of v1, /device:TPU:0, one launch (start us, length us, event | category | flops | bytes accessed | tf_op | source)
XLA Modules:
  0.0 56.3 jit_solution(8346382416522531208)
XLA Ops:
  0.0 2.9 %copy-done = bf16[640,5120]{1,0:T(8,128)(2,1)S(1)} copy-done((bf16[640,5120]{1,0:T(8,128)(2,1)S(1)}, bf16[640,5120]{1,0:T(8,128)(2,1)}, u32[]{:S(2)}) %copy-start) | copy-done | bytes 6553624
  2.9 0.9 %split_weights.1 = (bf16[640,2560]{1,0:T(8,128)(2,1)S(1)}, bf16[640,2560]{1,0:T(8,128)(2,1)S(1)}) custom-call(bf16[640,5120]{1,0:T(8,128)(2,1)S(1)} %copy-done), custom_call_target="tpu_custom_call" | custom-call | bytes 13107200 | tf_op jit(solution)/shard_map/split_weights/pallas_call | solution.py:109
  3.8 0.6 collective-permute-start.15
  4.3 2.6 %collective-permute-start = (bf16[160,640]{1,0:T(8,128)(2,1)S(1)}, bf16[160,640]{1,0:T(8,128)(2,1)S(1)}, u32[]{:S(2)}, u32[]{:S(2)}) collective-permute-start(bf16[160,640]{1,0:T(8,128)(2,1)S(1)} %copy-done.2), channel_id=1, source_target_pairs={{0,8},{8,16},{16,24},{24,28},{28,20},{20,12},{12,4},{4,0},{1,9},{9... | collective-permute-start | bytes 614408 | tf_op jit(solution)/shard_map/ppermute | solution.py:207
  7.0 2.0 %collective-permute-start.8 = (bf16[160,640]{1,0:T(8,128)(2,1)S(1)}, bf16[160,640]{1,0:T(8,128)(2,1)S(1)}, u32[]{:S(2)}, u32[]{:S(2)}) collective-permute-start(bf16[160,640]{1,0:T(8,128)(2,1)S(1)} %copy-done.2), channel_id=1, source_target_pairs={{8,0},{16,8},{24,16},{28,24},{20,28},{12,20},{4,12},{0,4},{9,1},{1... | collective-permute-start | bytes 614408 | tf_op jit(solution)/shard_map/ppermute | solution.py:210
  9.0 3.8 %collective-permute-done.refs_1_ = bf16[160,640]{1,0:T(8,128)(2,1)S(1)} collective-permute-done((bf16[160,640]{1,0:T(8,128)(2,1)S(1)}, bf16[160,640]{1,0:T(8,128)(2,1)S(1)}, u32[]{:S(2)}, u32[]{:S(2)}) %collective-permute-start) | collective-permute-done | bytes 204832 | tf_op jit(solution)/shard_map/ppermute | solution.py:207
  12.8 2.1 %collective-permute-start.1 = (bf16[160,640]{1,0:T(8,128)(2,1)S(1)}, bf16[160,640]{1,0:T(8,128)(2,1)S(1)}, u32[]{:S(2)}, u32[]{:S(2)}) collective-permute-start(bf16[160,640]{1,0:T(8,128)(2,1)S(1)} %collective-permute-done.refs_1_), channel_id=1, source_target_pairs={{0,8},{8,16},{16,24},{24,28},{28,20},{20,12},{12,4},{4,0},{1,9},{9... | collective-permute-start | bytes 614408 | tf_op jit(solution)/shard_map/ppermute | solution.py:207
  14.9 4.4 %collective-permute-done.8.refs_2_ = bf16[160,640]{1,0:T(8,128)(2,1)S(1)} collective-permute-done((bf16[160,640]{1,0:T(8,128)(2,1)S(1)}, bf16[160,640]{1,0:T(8,128)(2,1)S(1)}, u32[]{:S(2)}, u32[]{:S(2)}) %collective-permute-start.8) | collective-permute-done | bytes 204832 | tf_op jit(solution)/shard_map/ppermute | solution.py:210
  19.3 2.0 %collective-permute-start.12 = (bf16[160,640]{1,0:T(8,128)(2,1)S(1)}, bf16[160,640]{1,0:T(8,128)(2,1)S(1)}, u32[]{:S(2)}, u32[]{:S(2)}) collective-permute-start(bf16[160,640]{1,0:T(8,128)(2,1)S(1)} %collective-permute-done.11.refs_3_), channel_id=1, source_target_pairs={{0,8},{8,16},{16,24},{24,28},{28,20},{20,12},{12,4},{4,0},{1,9},{9... | collective-permute-start | bytes 614408 | tf_op jit(solution)/shard_map/ppermute | solution.py:209
  21.6 2.1 %collective-permute-start.2 = (bf16[160,640]{1,0:T(8,128)(2,1)S(1)}, bf16[160,640]{1,0:T(8,128)(2,1)S(1)}, u32[]{:S(2)}, u32[]{:S(2)}) collective-permute-start(bf16[160,640]{1,0:T(8,128)(2,1)S(1)} %collective-permute-done.1.refs_1_), channel_id=1, source_target_pairs={{0,8},{8,16},{16,24},{24,28},{28,20},{20,12},{12,4},{4,0},{1,9},{9... | collective-permute-start | bytes 614408 | tf_op jit(solution)/shard_map/ppermute | solution.py:207
  23.7 4.4 %collective-permute-done.9.refs_2_ = bf16[160,640]{1,0:T(8,128)(2,1)S(1)} collective-permute-done((bf16[160,640]{1,0:T(8,128)(2,1)S(1)}, bf16[160,640]{1,0:T(8,128)(2,1)S(1)}, u32[]{:S(2)}, u32[]{:S(2)}) %collective-permute-start.9) | collective-permute-done | bytes 204832 | tf_op jit(solution)/shard_map/ppermute | solution.py:210
  28.1 2.0 %collective-permute-start.13 = (bf16[160,640]{1,0:T(8,128)(2,1)S(1)}, bf16[160,640]{1,0:T(8,128)(2,1)S(1)}, u32[]{:S(2)}, u32[]{:S(2)}) collective-permute-start(bf16[160,640]{1,0:T(8,128)(2,1)S(1)} %collective-permute-done.12.refs_3_), channel_id=1, source_target_pairs={{0,8},{8,16},{16,24},{24,28},{28,20},{20,12},{12,4},{4,0},{1,9},{9... | collective-permute-start | bytes 614408 | tf_op jit(solution)/shard_map/ppermute | solution.py:209
  30.1 0.7 %collective-permute-done.2.refs_1_ = bf16[160,640]{1,0:T(8,128)(2,1)S(1)} collective-permute-done((bf16[160,640]{1,0:T(8,128)(2,1)S(1)}, bf16[160,640]{1,0:T(8,128)(2,1)S(1)}, u32[]{:S(2)}, u32[]{:S(2)}) %collective-permute-start.2) | collective-permute-done | bytes 204832 | tf_op jit(solution)/shard_map/ppermute | solution.py:207
  30.8 2.1 %collective-permute-start.3 = (bf16[160,640]{1,0:T(8,128)(2,1)S(1)}, bf16[160,640]{1,0:T(8,128)(2,1)S(1)}, u32[]{:S(2)}, u32[]{:S(2)}) collective-permute-start(bf16[160,640]{1,0:T(8,128)(2,1)S(1)} %collective-permute-done.2.refs_1_), channel_id=1, source_target_pairs={{0,8},{8,16},{16,24},{24,28},{28,20},{20,12},{12,4},{4,0},{1,9},{9... | collective-permute-start | bytes 614408 | tf_op jit(solution)/shard_map/ppermute | solution.py:212
  33.0 0.8 %flash.5 = (f32[160,640]{1,0:T(8,128)S(1)}, f32[160,640]{1,0:T(8,128)S(1)}, f32[160,640]{1,0:T(8,128)S(1)}) custom-call(bf16[160,640]{1,0:T(8,128)(2,1)S(1)} %copy-done.1, bf16[160,640]{1,0:T(8,128)(2,1)S(1)} %copy-done.2, bf16[160,640]{1,0:T(8,128)(2,1)S(1)} %copy-done.3), custom_call_target="tpu_custom_call" | custom-call | flops 65536000 | bytes 3072000 | tf_op jit(solution)/shard_map/flash/pallas_call | solution.py:72
  33.8 1.9 %flash.6 = (f32[160,640]{1,0:T(8,128)S(1)}, f32[160,640]{1,0:T(8,128)S(1)}, f32[160,640]{1,0:T(8,128)S(1)}) custom-call(bf16[160,640]{1,0:T(8,128)(2,1)S(1)} %copy-done.1, bf16[160,640]{1,0:T(8,128)(2,1)S(1)} %collective-permute-done.refs_1_, bf16[160,640]{1,0:T(8,128)(2,1)S(1)} %collective-permute-done.8.refs_2_, ...), custom_call_target="tpu_custom_call" | custom-call | flops 131072000 | bytes 3481600 | tf_op jit(solution)/shard_map/flash/pallas_call | solution.py:72
  35.6 1.9 %flash.7 = (f32[160,640]{1,0:T(8,128)S(1)}, f32[160,640]{1,0:T(8,128)S(1)}, f32[160,640]{1,0:T(8,128)S(1)}) custom-call(bf16[160,640]{1,0:T(8,128)(2,1)S(1)} %copy-done.1, bf16[160,640]{1,0:T(8,128)(2,1)S(1)} %collective-permute-done.1.refs_1_, bf16[160,640]{1,0:T(8,128)(2,1)S(1)} %collective-permute-done.9.refs_2_, ...), custom_call_target="tpu_custom_call" | custom-call | flops 131072000 | bytes 3481600 | tf_op jit(solution)/shard_map/flash/pallas_call | solution.py:72
  37.5 1.9 %flash.8 = (f32[160,640]{1,0:T(8,128)S(1)}, f32[160,640]{1,0:T(8,128)S(1)}, f32[160,640]{1,0:T(8,128)S(1)}) custom-call(bf16[160,640]{1,0:T(8,128)(2,1)S(1)} %copy-done.1, bf16[160,640]{1,0:T(8,128)(2,1)S(1)} %collective-permute-done.2.refs_1_, bf16[160,640]{1,0:T(8,128)(2,1)S(1)} %collective-permute-done.10.refs_2_, ...), custom_call_target="tpu_custom_call" | custom-call | flops 131072000 | bytes 3481600 | tf_op jit(solution)/shard_map/flash/pallas_call | solution.py:72
  39.4 1.1 %collective-permute-done.7.refs_2_ = bf16[160,640]{1,0:T(8,128)(2,1)S(1)} collective-permute-done((bf16[160,640]{1,0:T(8,128)(2,1)S(1)}, bf16[160,640]{1,0:T(8,128)(2,1)S(1)}, u32[]{:S(2)}, u32[]{:S(2)}) %collective-permute-start.7) | collective-permute-done | bytes 204832 | tf_op jit(solution)/shard_map/ppermute | solution.py:213
  40.5 1.6 %flash.9.a_ref = bf16[160,640]{1,0:T(8,128)(2,1)S(1)} custom-call(bf16[160,640]{1,0:T(8,128)(2,1)S(1)} %copy-done.1, bf16[160,640]{1,0:T(8,128)(2,1)S(1)} %collective-permute-done.3.refs_1_, bf16[160,640]{1,0:T(8,128)(2,1)S(1)} %collective-permute-done.7.refs_2_, f32[160,640]{1,0:T(8,128)S(1)} %get-tuple-element.28.refs_3_, ...), custom_call_target="tpu_custom_call" | custom-call | flops 65536000 | bytes 3072000 | tf_op jit(solution)/shard_map/flash/pallas_call | solution.py:72
  42.1 0.4 project.14.refs_0_
  42.5 0.4 project.10.refs_0_
  43.0 0.6 %collective-permute-done.14.a_ref = bf16[160,640]{1,0:T(8,128)(2,1)S(1)} collective-permute-done((bf16[160,640]{1,0:T(8,128)(2,1)S(1)}, bf16[160,640]{1,0:T(8,128)(2,1)S(1)}, u32[]{:S(2)}, u32[]{:S(2)}) %collective-permute-start.14) | collective-permute-done | bytes 204832 | tf_op jit(solution)/shard_map/ppermute | solution.py:215
  43.6 0.4 project.15
  44.0 1.6 %collective-permute-start.17 = (bf16[160,640]{1,0:T(8,128)(2,1)S(1)}, bf16[160,640]{1,0:T(8,128)(2,1)S(1)}, u32[]{:S(2)}, u32[]{:S(2)}) collective-permute-start(bf16[160,640]{1,0:T(8,128)(2,1)S(1)} %project.15), channel_id=1, source_target_pairs={{0,2},{1,3},{2,0},{3,1},{4,6},{5,7},{6,4},{7,5},{8,10},{9,11},{10,... | collective-permute-start | bytes 614408 | tf_op jit(solution)/shard_map/ppermute | solution.py:224
  45.5 0.4 project.11
  46.0 0.6 %collective-permute-start.16 = (bf16[160,640]{1,0:T(8,128)(2,1)S(1)}, bf16[160,640]{1,0:T(8,128)(2,1)S(1)}, u32[]{:S(2)}, u32[]{:S(2)}) collective-permute-start(bf16[160,640]{1,0:T(8,128)(2,1)S(1)} %project.11), channel_id=1, source_target_pairs={{0,2},{1,3},{2,0},{3,1},{4,6},{5,7},{6,4},{7,5},{8,10},{9,11},{10,... | collective-permute-start | bytes 614408 | tf_op jit(solution)/shard_map/ppermute | solution.py:224
  47.0 0.4 project.8.refs_0_
  48.3 3.7 %collective-permute-done.17.refs_1_ = bf16[160,640]{1,0:T(8,128)(2,1)S(1)} collective-permute-done((bf16[160,640]{1,0:T(8,128)(2,1)S(1)}, bf16[160,640]{1,0:T(8,128)(2,1)S(1)}, u32[]{:S(2)}, u32[]{:S(2)}) %collective-permute-start.17) | collective-permute-done | bytes 204832 | tf_op jit(solution)/shard_map/ppermute | solution.py:224
  52.0 0.7 %finish.2.refs_2_ = bf16[160,1280]{1,0:T(8,128)(2,1)} custom-call(f32[160,640]{1,0:T(8,128)S(1)} %project.13.refs_0_, bf16[160,640]{1,0:T(8,128)(2,1)S(1)} %collective-permute-done.17.refs_1_), custom_call_target="tpu_custom_call" | custom-call | flops 102400 | bytes 819200 | tf_op jit(solution)/shard_map/finish/pallas_call | solution.py:171
  52.7 2.8 %collective-permute-done.16.refs_1_ = bf16[160,640]{1,0:T(8,128)(2,1)S(1)} collective-permute-done((bf16[160,640]{1,0:T(8,128)(2,1)S(1)}, bf16[160,640]{1,0:T(8,128)(2,1)S(1)}, u32[]{:S(2)}, u32[]{:S(2)}) %collective-permute-start.16) | collective-permute-done | bytes 204832 | tf_op jit(solution)/shard_map/ppermute | solution.py:224
  55.6 0.7 %finish.3 = bf16[160,1280]{1,0:T(8,128)(2,1)} custom-call(f32[160,640]{1,0:T(8,128)S(1)} %project.9.refs_0_, bf16[160,640]{1,0:T(8,128)(2,1)S(1)} %collective-permute-done.16.refs_1_, bf16[160,1280]{1,0:T(8,128)(2,1)} %finish.2.refs_2_), custom_call_target="tpu_custom_call", output_to_operand_aliasing={{}: (2, {})} | custom-call | flops 102400 | bytes 819200 | tf_op jit(solution)/shard_map/finish/pallas_call | solution.py:171
  (28 shorter events, 1.8 us)
Async XLA Ops:
  0.0 2.9 %copy-start = (bf16[640,5120]{1,0:T(8,128)(2,1)S(1)}, bf16[640,5120]{1,0:T(8,128)(2,1)}, u32[]{:S(2)}) copy-start(bf16[640,5120]{1,0:T(8,128)(2,1)} %w_ref.1) | copy-start | bytes 19660804
  2.9 1.5 %copy-start.2 = (bf16[160,640]{1,0:T(8,128)(2,1)S(1)}, bf16[160,640]{1,0:T(8,128)(2,1)}, u32[]{:S(2)}) copy-start(bf16[160,640]{1,0:T(8,128)(2,1)} %refs_1_.1) | copy-start | bytes 614404
  2.9 4.1 %copy-start.3 = (bf16[160,640]{1,0:T(8,128)(2,1)S(1)}, bf16[160,640]{1,0:T(8,128)(2,1)}, u32[]{:S(2)}) copy-start(bf16[160,640]{1,0:T(8,128)(2,1)} %refs_2_.1) | copy-start | bytes 614404
  2.9 30.1 %copy-start.1 = (bf16[160,640]{1,0:T(8,128)(2,1)S(1)}, bf16[160,640]{1,0:T(8,128)(2,1)}, u32[]{:S(2)}) copy-start(bf16[160,640]{1,0:T(8,128)(2,1)} %refs_0_.9) | copy-start | bytes 614404
  3.8 39.8 %collective-permute-start.15 = (bf16[640,2560]{1,0:T(8,128)(2,1)S(1)}, bf16[640,2560]{1,0:T(8,128)(2,1)S(1)}, u32[]{:S(2)}, u32[]{:S(2)}) collective-permute-start(bf16[640,2560]{1,0:T(8,128)(2,1)S(1)} %get-tuple-element.31), channel_id=1, source_target_pairs={{0,1},{1,0},{2,3},{3,2},{4,5},{5,4},{6,7},{7,6},{8,9},{9,8},{10,11... | collective-permute-start | bytes 9830408 | tf_op jit(solution)/shard_map/ppermute | solution.py:202
  4.3 8.5 %collective-permute-start = (bf16[160,640]{1,0:T(8,128)(2,1)S(1)}, bf16[160,640]{1,0:T(8,128)(2,1)S(1)}, u32[]{:S(2)}, u32[]{:S(2)}) collective-permute-start(bf16[160,640]{1,0:T(8,128)(2,1)S(1)} %copy-done.2), channel_id=1, source_target_pairs={{0,8},{8,16},{16,24},{24,28},{28,20},{20,12},{12,4},{4,0},{1,9},{9... | collective-permute-start | bytes 614408 | tf_op jit(solution)/shard_map/ppermute | solution.py:207
  7.0 8.0 %collective-permute-start.4 = (bf16[160,640]{1,0:T(8,128)(2,1)S(1)}, bf16[160,640]{1,0:T(8,128)(2,1)S(1)}, u32[]{:S(2)}, u32[]{:S(2)}) collective-permute-start(bf16[160,640]{1,0:T(8,128)(2,1)S(1)} %copy-done.3), channel_id=1, source_target_pairs={{8,0},{16,8},{24,16},{28,24},{20,28},{12,20},{4,12},{0,4},{9,1},{1... | collective-permute-start | bytes 614408 | tf_op jit(solution)/shard_map/ppermute | solution.py:208
  7.0 12.3 %collective-permute-start.8 = (bf16[160,640]{1,0:T(8,128)(2,1)S(1)}, bf16[160,640]{1,0:T(8,128)(2,1)S(1)}, u32[]{:S(2)}, u32[]{:S(2)}) collective-permute-start(bf16[160,640]{1,0:T(8,128)(2,1)S(1)} %copy-done.2), channel_id=1, source_target_pairs={{8,0},{16,8},{24,16},{28,24},{20,28},{12,20},{4,12},{0,4},{9,1},{1... | collective-permute-start | bytes 614408 | tf_op jit(solution)/shard_map/ppermute | solution.py:210
  8.9 10.4 %collective-permute-start.11 = (bf16[160,640]{1,0:T(8,128)(2,1)S(1)}, bf16[160,640]{1,0:T(8,128)(2,1)S(1)}, u32[]{:S(2)}, u32[]{:S(2)}) collective-permute-start(bf16[160,640]{1,0:T(8,128)(2,1)S(1)} %copy-done.3), channel_id=1, source_target_pairs={{0,8},{8,16},{16,24},{24,28},{28,20},{20,12},{12,4},{4,0},{1,9},{9... | collective-permute-start | bytes 614408 | tf_op jit(solution)/shard_map/ppermute | solution.py:209
  12.8 8.8 %collective-permute-start.1 = (bf16[160,640]{1,0:T(8,128)(2,1)S(1)}, bf16[160,640]{1,0:T(8,128)(2,1)S(1)}, u32[]{:S(2)}, u32[]{:S(2)}) collective-permute-start(bf16[160,640]{1,0:T(8,128)(2,1)S(1)} %collective-permute-done.refs_1_), channel_id=1, source_target_pairs={{0,8},{8,16},{16,24},{24,28},{28,20},{20,12},{12,4},{4,0},{1,9},{9... | collective-permute-start | bytes 614408 | tf_op jit(solution)/shard_map/ppermute | solution.py:207
  14.9 8.8 %collective-permute-start.5 = (bf16[160,640]{1,0:T(8,128)(2,1)S(1)}, bf16[160,640]{1,0:T(8,128)(2,1)S(1)}, u32[]{:S(2)}, u32[]{:S(2)}) collective-permute-start(bf16[160,640]{1,0:T(8,128)(2,1)S(1)} %collective-permute-done.4.refs_4_), channel_id=1, source_target_pairs={{8,0},{16,8},{24,16},{28,24},{20,28},{12,20},{4,12},{0,4},{9,1},{1... | collective-permute-start | bytes 614408 | tf_op jit(solution)/shard_map/ppermute | solution.py:208
  19.3 8.8 %collective-permute-start.9 = (bf16[160,640]{1,0:T(8,128)(2,1)S(1)}, bf16[160,640]{1,0:T(8,128)(2,1)S(1)}, u32[]{:S(2)}, u32[]{:S(2)}) collective-permute-start(bf16[160,640]{1,0:T(8,128)(2,1)S(1)} %collective-permute-done.8.refs_2_), channel_id=1, source_target_pairs={{8,0},{16,8},{24,16},{28,24},{20,28},{12,20},{4,12},{0,4},{9,1},{1... | collective-permute-start | bytes 614408 | tf_op jit(solution)/shard_map/ppermute | solution.py:210
  19.3 8.8 %collective-permute-start.12 = (bf16[160,640]{1,0:T(8,128)(2,1)S(1)}, bf16[160,640]{1,0:T(8,128)(2,1)S(1)}, u32[]{:S(2)}, u32[]{:S(2)}) collective-permute-start(bf16[160,640]{1,0:T(8,128)(2,1)S(1)} %collective-permute-done.11.refs_3_), channel_id=1, source_target_pairs={{0,8},{8,16},{16,24},{24,28},{28,20},{20,12},{12,4},{4,0},{1,9},{9... | collective-permute-start | bytes 614408 | tf_op jit(solution)/shard_map/ppermute | solution.py:209
  21.6 9.2 %collective-permute-start.2 = (bf16[160,640]{1,0:T(8,128)(2,1)S(1)}, bf16[160,640]{1,0:T(8,128)(2,1)S(1)}, u32[]{:S(2)}, u32[]{:S(2)}) collective-permute-start(bf16[160,640]{1,0:T(8,128)(2,1)S(1)} %collective-permute-done.1.refs_1_), channel_id=1, source_target_pairs={{0,8},{8,16},{16,24},{24,28},{28,20},{20,12},{12,4},{4,0},{1,9},{9... | collective-permute-start | bytes 614408 | tf_op jit(solution)/shard_map/ppermute | solution.py:207
  23.7 9.3 %collective-permute-start.6 = (bf16[160,640]{1,0:T(8,128)(2,1)S(1)}, bf16[160,640]{1,0:T(8,128)(2,1)S(1)}, u32[]{:S(2)}, u32[]{:S(2)}) collective-permute-start(bf16[160,640]{1,0:T(8,128)(2,1)S(1)} %collective-permute-done.5.refs_4_), channel_id=1, source_target_pairs={{8,0},{16,8},{24,16},{28,24},{20,28},{12,20},{4,12},{0,4},{9,1},{1... | collective-permute-start | bytes 614408 | tf_op jit(solution)/shard_map/ppermute | solution.py:208
  28.1 9.4 %collective-permute-start.10 = (bf16[160,640]{1,0:T(8,128)(2,1)S(1)}, bf16[160,640]{1,0:T(8,128)(2,1)S(1)}, u32[]{:S(2)}, u32[]{:S(2)}) collective-permute-start(bf16[160,640]{1,0:T(8,128)(2,1)S(1)} %collective-permute-done.9.refs_2_), channel_id=1, source_target_pairs={{8,0},{16,8},{24,16},{28,24},{20,28},{12,20},{4,12},{0,4},{9,1},{1... | collective-permute-start | bytes 614408 | tf_op jit(solution)/shard_map/ppermute | solution.py:210
  28.1 9.4 %collective-permute-start.13 = (bf16[160,640]{1,0:T(8,128)(2,1)S(1)}, bf16[160,640]{1,0:T(8,128)(2,1)S(1)}, u32[]{:S(2)}, u32[]{:S(2)}) collective-permute-start(bf16[160,640]{1,0:T(8,128)(2,1)S(1)} %collective-permute-done.12.refs_3_), channel_id=1, source_target_pairs={{0,8},{8,16},{16,24},{24,28},{28,20},{20,12},{12,4},{4,0},{1,9},{9... | collective-permute-start | bytes 614408 | tf_op jit(solution)/shard_map/ppermute | solution.py:209
  30.8 8.5 %collective-permute-start.3 = (bf16[160,640]{1,0:T(8,128)(2,1)S(1)}, bf16[160,640]{1,0:T(8,128)(2,1)S(1)}, u32[]{:S(2)}, u32[]{:S(2)}) collective-permute-start(bf16[160,640]{1,0:T(8,128)(2,1)S(1)} %collective-permute-done.2.refs_1_), channel_id=1, source_target_pairs={{0,8},{8,16},{16,24},{24,28},{28,20},{20,12},{12,4},{4,0},{1,9},{9... | collective-permute-start | bytes 614408 | tf_op jit(solution)/shard_map/ppermute | solution.py:212
  33.0 7.5 %collective-permute-start.7 = (bf16[160,640]{1,0:T(8,128)(2,1)S(1)}, bf16[160,640]{1,0:T(8,128)(2,1)S(1)}, u32[]{:S(2)}, u32[]{:S(2)}) collective-permute-start(bf16[160,640]{1,0:T(8,128)(2,1)S(1)} %collective-permute-done.6.refs_4_), channel_id=1, source_target_pairs={{8,0},{16,8},{24,16},{28,24},{20,28},{12,20},{4,12},{0,4},{9,1},{1... | collective-permute-start | bytes 614408 | tf_op jit(solution)/shard_map/ppermute | solution.py:213
  42.0 1.5 %collective-permute-start.14 = (bf16[160,640]{1,0:T(8,128)(2,1)S(1)}, bf16[160,640]{1,0:T(8,128)(2,1)S(1)}, u32[]{:S(2)}, u32[]{:S(2)}) collective-permute-start(bf16[160,640]{1,0:T(8,128)(2,1)S(1)} %flash.9.a_ref), channel_id=1, source_target_pairs={{0,1},{1,0},{2,3},{3,2},{4,5},{5,4},{6,7},{7,6},{8,9},{9,8},{10,11... | collective-permute-start | bytes 614408 | tf_op jit(solution)/shard_map/ppermute | solution.py:215
  44.0 8.0 %collective-permute-start.17 = (bf16[160,640]{1,0:T(8,128)(2,1)S(1)}, bf16[160,640]{1,0:T(8,128)(2,1)S(1)}, u32[]{:S(2)}, u32[]{:S(2)}) collective-permute-start(bf16[160,640]{1,0:T(8,128)(2,1)S(1)} %project.15), channel_id=1, source_target_pairs={{0,2},{1,3},{2,0},{3,1},{4,6},{5,7},{6,4},{7,5},{8,10},{9,11},{10,... | collective-permute-start | bytes 614408 | tf_op jit(solution)/shard_map/ppermute | solution.py:224
  46.0 9.6 %collective-permute-start.16 = (bf16[160,640]{1,0:T(8,128)(2,1)S(1)}, bf16[160,640]{1,0:T(8,128)(2,1)S(1)}, u32[]{:S(2)}, u32[]{:S(2)}) collective-permute-start(bf16[160,640]{1,0:T(8,128)(2,1)S(1)} %project.11), channel_id=1, source_target_pairs={{0,2},{1,3},{2,0},{3,1},{4,6},{5,7},{6,4},{7,5},{8,10},{9,11},{10,... | collective-permute-start | bytes 614408 | tf_op jit(solution)/shard_map/ppermute | solution.py:224

commit v2 on v1

v2 whole, which is shorter than its diff:
```python
import functools
import math

import jax
import jax.numpy as jnp
from jax import lax
from jax.experimental import pallas as pl
from jax.experimental.pallas import tpu as pltpu
from jax.sharding import PartitionSpec as P


HD = 128
VM = pl.BlockSpec(memory_space=pltpu.VMEM)
GRANT = 8 * 2**20
PIECE = 512


def params():
    return pltpu.CompilerParams(vmem_limit_bytes=GRANT)


def flash_kernel(heads, blocks, first, *refs):
    q_ref = refs[0]
    k_refs = refs[1 : 1 + blocks]
    v_refs = refs[1 + blocks : 1 + 2 * blocks]
    rest = refs[1 + 2 * blocks :]
    rows = q_ref.shape[0]
    if not first:
        acc_in, top_in, total_in = rest[:3]
        rest = rest[3:]
    acc_ref, top_ref, total_ref = rest
    for h in range(heads):
        cols = slice(h * HD, (h + 1) * HD)
        key = jnp.concatenate([ref[:, cols] for ref in k_refs], axis=0)
        value = jnp.concatenate([ref[:, cols] for ref in v_refs], axis=0)
        scores = score(q_ref[:, cols], key)
        top = jnp.broadcast_to(jnp.max(scores, axis=1, keepdims=True), (rows, HD))
        if not first:
            old_top = top_in[:, cols]
            top = jnp.maximum(top, old_top)
        expo = jnp.exp2(scores - top[:, :1])
        total = jnp.broadcast_to(jnp.sum(expo, axis=1, keepdims=True), (rows, HD))
        summed = jnp.dot(expo.astype(jnp.bfloat16), value, preferred_element_type=jnp.float32)
        if not first:
            shrink = jnp.exp2(old_top - top)
            total = total + shrink * total_in[:, cols]
            summed = summed + shrink * acc_in[:, cols]
        acc_ref[:, cols] = summed
        top_ref[:, cols] = top
        total_ref[:, cols] = total


def score(query, key):
    factor = math.log2(math.e) / math.sqrt(HD)
    return factor * lax.dot_general(
        query, key, (((1,), (1,)), ((), ())), preferred_element_type=jnp.float32
    )


def flash(query, keys, values, state):
    rows, width = query.shape
    heads = width // HD
    blocks = len(keys)
    count = sum(k.shape[0] for k in keys)
    args = (query, *keys, *values, *state)
    return pl.pallas_call(
        functools.partial(flash_kernel, heads, blocks, not state),
        out_shape=[jax.ShapeDtypeStruct((rows, width), jnp.float32)] * 3,
        in_specs=[VM] * len(args),
        out_specs=[VM] * 3,
        cost_estimate=pl.CostEstimate(
            flops=4 * rows * count * width,
            transcendentals=rows * count * heads,
            bytes_accessed=2 * rows * width * (1 + 2 * blocks) + 24 * rows * width,
        ),
        compiler_params=params(),
        name="flash",
    )(*args)


def last_scores_kernel(heads, q_ref, k_ref, acc_in, top_in, total_in, expo_ref, acc_ref, norm_ref):
    rows = q_ref.shape[0]
    for h in range(heads):
        cols = slice(h * HD, (h + 1) * HD)
        scores = score(q_ref[:, cols], k_ref[:, cols])
        old_top = top_in[:, cols]
        top = jnp.broadcast_to(jnp.max(scores, axis=1, keepdims=True), (rows, HD))
        top = jnp.maximum(top, old_top)
        expo = jnp.exp2(scores - top[:, :1])
        total = jnp.broadcast_to(jnp.sum(expo, axis=1, keepdims=True), (rows, HD))
        shrink = jnp.exp2(old_top - top)
        norm = jnp.exp2(-jnp.log2(total + shrink * total_in[:, cols]))
        expo_ref[h] = expo.astype(jnp.bfloat16)
        acc_ref[:, cols] = acc_in[:, cols] * (shrink * norm)
        norm_ref[:, cols] = norm


def last_scores(query, keys, state):
    rows, width = query.shape
    heads = width // HD
    count = keys.shape[0]
    wide = jax.ShapeDtypeStruct((rows, width), jnp.float32)
    return pl.pallas_call(
        functools.partial(last_scores_kernel, heads),
        out_shape=(jax.ShapeDtypeStruct((heads, rows, count), jnp.bfloat16), wide, wide),
        in_specs=[VM] * 5,
        out_specs=(VM,) * 3,
        cost_estimate=pl.CostEstimate(
            flops=2 * rows * count * width,
            transcendentals=rows * count * heads,
            bytes_accessed=24 * rows * width,
        ),
        compiler_params=params(),
        name="last_scores",
    )(query, keys, *state)


def last_values_kernel(heads, expo_ref, v_ref, acc_ref, norm_ref, out_ref):
    for h in range(heads):
        cols = slice(h * HD, (h + 1) * HD)
        summed = jnp.dot(expo_ref[h], v_ref[:, cols], preferred_element_type=jnp.float32)
        out_ref[:, cols] = (acc_ref[:, cols] + summed * norm_ref[:, cols]).astype(out_ref.dtype)


def last_values(expo, values, acc, norm):
    heads, rows, count = expo.shape
    width = heads * HD
    return pl.pallas_call(
        functools.partial(last_values_kernel, heads),
        out_shape=jax.ShapeDtypeStruct((rows, width), jnp.bfloat16),
        in_specs=[VM] * 4,
        out_specs=VM,
        cost_estimate=pl.CostEstimate(
            flops=2 * rows * count * width, transcendentals=0, bytes_accessed=14 * rows * width
        ),
        compiler_params=params(),
        name="last_values",
    )(expo, values, acc, norm)


def weights_kernel(chips, columns, w_ref, mine_ref, other_ref, sems):
    place = lax.axis_index("head")
    copies = []
    for p in range(chips):
        target = lax.rem(place // 2 + p + 1, chips)
        for side, out in enumerate((mine_ref, other_ref)):
            core = place % 2 if side == 0 else 1 - place % 2
            start = pl.multiple_of((2 * target + core) * columns, HD)
            copy = pltpu.make_async_copy(
                w_ref.at[:, pl.ds(start, columns)],
                out.at[:, pl.ds(p * columns, columns)],
                sems.at[2 * p + side],
            )
            copy.start()
            copies.append(copy)
    for copy in copies:
        copy.wait()


def split_weights(weight, chips, columns):
    depth = weight.shape[0]
    half = jax.ShapeDtypeStruct((depth, chips * columns), weight.dtype)
    return pl.pallas_call(
        functools.partial(weights_kernel, chips, columns),
        out_shape=(half, half),
        in_specs=[pl.BlockSpec(memory_space=pl.ANY)],
        out_specs=(VM, VM),
        scratch_shapes=[pltpu.SemaphoreType.DMA((2 * chips,))],
        cost_estimate=pl.CostEstimate(
            flops=0, transcendentals=0, bytes_accessed=8 * depth * chips * columns
        ),
        compiler_params=pltpu.CompilerParams(vmem_limit_bytes=2 * GRANT),
        name="split_weights",
    )(weight)


def project_kernel(first, tile, skip, a_ref, w_ref, *refs):
    out_ref = refs[-1]
    for start in range(0, out_ref.shape[1], tile):
        value = jnp.dot(
            a_ref[...],
            w_ref[:, first + start : first + start + tile],
            preferred_element_type=jnp.float32,
        )
        if len(refs) > 1:
            value = value + refs[0][:, skip + start : skip + start + tile]
        out_ref[:, start : start + tile] = value.astype(out_ref.dtype)


def project(rows_in, weight, first, columns, base, skip, dtype):
    rows, depth = rows_in.shape
    tile = 256 if columns % 256 == 0 else HD
    args = (rows_in, weight) if base is None else (rows_in, weight, base)
    return pl.pallas_call(
        functools.partial(project_kernel, first, tile, skip),
        out_shape=jax.ShapeDtypeStruct((rows, columns), dtype),
        in_specs=[VM] * len(args),
        out_specs=VM,
        cost_estimate=pl.CostEstimate(
            flops=2 * rows * depth * columns,
            transcendentals=0,
            bytes_accessed=2 * depth * columns + 4 * rows * columns,
        ),
        compiler_params=params(),
        name="project",
    )(*args)


def finish_kernel(skip, arrived, *refs):
    columns = refs[-1].shape[1]
    total = refs[0][:, skip : skip + columns]
    for ref in refs[1 : 1 + arrived]:
        total = total + ref[...].astype(jnp.float32)
    refs[-1][...] = total.astype(refs[-1].dtype)


def finish(mine, parts, start, columns, output):
    rows = mine.shape[0]
    args = (mine, *parts)
    specs = [VM] * len(args)
    aliases = {}
    if output is not None:
        aliases = {len(args): 0}
        args += (output,)
        specs.append(pl.BlockSpec(memory_space=pl.ANY))
    return pl.pallas_call(
        functools.partial(finish_kernel, start, len(parts)),
        out_shape=jax.ShapeDtypeStruct(mine.shape, jnp.bfloat16),
        grid=(1,),
        in_specs=specs,
        out_specs=pl.BlockSpec((rows, columns), lambda i: (0, start // columns)),
        input_output_aliases=aliases,
        cost_estimate=pl.CostEstimate(
            flops=rows * columns, transcendentals=0, bytes_accessed=8 * rows * columns
        ),
        compiler_params=params(),
        name="finish",
    )(*args)


def column_pieces(columns):
    narrow = columns % PIECE or PIECE
    return [(columns - narrow, narrow)] + [(c, PIECE) for c in range(0, columns - narrow, PIECE)]


def ring_pairs(n):
    order = list(range(0, n, 2)) + list(range(1, n, 2))[::-1]
    ahead = [(order[i], order[(i + 1) % n]) for i in range(n)]
    return ahead, [(b, a) for a, b in ahead]


def on_device(n_seq, n_head, queries, keys, values, out_weight):
    ahead, back = ring_pairs(n_seq)
    columns = out_weight.shape[1] // n_head
    chips = n_head // 2
    swap = [(i, i ^ 1) for i in range(n_head)]
    pieces = column_pieces(columns)
    steps = n_seq // 2

    w_mine, w_give = split_weights(out_weight, chips, columns)
    w_partner = lax.ppermute(w_give, "head", swap)
    state = flash(queries, [keys], [values], ())
    kf = kb = keys
    vf = vb = values
    for _ in range(1, steps):
        kf = lax.ppermute(kf, "seq", ahead)
        vb = lax.ppermute(vb, "seq", back)
        vf = lax.ppermute(vf, "seq", ahead)
        kb = lax.ppermute(kb, "seq", back)
        state = flash(queries, [kf, kb], [vf, vb], state)
    kf = lax.ppermute(kf, "seq", ahead)
    vb = lax.ppermute(vb, "seq", back)
    expo, acc, norm = last_scores(queries, kf, state)
    attended = last_values(expo, vb, acc, norm)
    partner = lax.ppermute(attended, "head", swap)

    away = (chips - 1) * columns
    part = project(attended, w_mine, 0, away, None, 0, jnp.float32)
    arrived = [[] for _ in pieces]
    for index, (start, piece) in enumerate(pieces):
        for hop in range(1, chips):
            pairs = [(i, (i + 2 * hop) % n_head) for i in range(n_head)]
            first = (hop - 1) * columns + start
            given = project(partner, w_partner, first, piece, part, first, jnp.bfloat16)
            arrived[index].append(lax.ppermute(given, "head", pairs))
    total = project(attended, w_mine, away, columns, None, 0, jnp.float32)
    total = project(partner, w_partner, away, columns, total, 0, jnp.float32)
    output = None
    for index, (start, piece) in enumerate(pieces):
        output = finish(total, arrived[index], start, piece, output)
    return output


def solution(mesh):
    n_seq, n_head = mesh.shape["seq"], mesh.shape["head"]
    placed = (P("seq", "head"), P("seq", "head"), P("seq", "head"), P("head", None))
    return jax.shard_map(
        functools.partial(on_device, n_seq, n_head),
        mesh=mesh,
        in_specs=placed,
        out_specs=P("seq", "head"),
        check_vma=False,
    )
```

time: 56.4 us -> 56.6 us (level)
  starting transfers between devices: 17.8 us -> 19.8 us
  waiting for transfers between devices: 21.8 us -> 20.6 us
  Pallas kernels: 13.6 us -> 12.9 us
    ppermute x2 -> x3, starting transfers between devices: 2.16 us -> 4.16 us  [on_device(): arrived[index].append(lax.ppermute(given, 'head', pairs))]
    ppermute x4, waiting for transfers between devices: 1.06 us -> 0.01 us  [on_device(): vb = lax.ppermute(vb, 'seq', back)]
    pallas_call x15, Pallas kernels: 12.7 us -> 12 us  [the longest x4 6.36 us: flash(): pl.pallas_call(functools.partial(flash_kernel, heads, blocks, not state),...]
    ppermute x2 -> x3, waiting for transfers between devices: 6.59 us -> 6.08 us  [on_device(): arrived[index].append(lax.ppermute(given, 'head', pairs))]
  transfers between devices with their start and end apart: 18 -> 19, of which waited for: 9 -> 7; matrix products, arithmetic and copies ran while one was open for 0% -> 0% of each run, Pallas kernels for 21% -> 20%
where the time goes in v2:
time: 56.6 us; the launch traced here: 56.4 us
  waiting for transfers between devices  20.6 us (36%)
  starting transfers between devices  19.8 us (35%)
  Pallas kernels  12.9 us (23%)
  local copies, waits for them, and re-layouts  2.87 us (5%)
    ppermute x4, starting transfers between devices, on_device(): kf = lax.ppermute(kf, 'seq', ahead)  8.91 us
    ppermute x3, waiting for transfers between devices, on_device(): kb = lax.ppermute(kb, 'seq', back)  8.75 us
    pallas_call x4, Pallas kernels, flash(): pl.pallas_call(functools.partial(flash_kernel, heads, blocks, not state),...  6.36 us
    ppermute x3, waiting for transfers between devices, on_device(): arrived[index].append(lax.ppermute(given, 'head', pairs))  6.08 us
    ppermute x4, waiting for transfers between devices, on_device(): kf = lax.ppermute(kf, 'seq', ahead)  4.82 us
    ppermute x3, starting transfers between devices, on_device(): arrived[index].append(lax.ppermute(given, 'head', pairs))  4.16 us
    ppermute x3, starting transfers between devices, on_device(): vf = lax.ppermute(vf, 'seq', ahead)  4.11 us
    unnamed x8, local copies, waits for them, and re-layouts  2.87 us
  transfers between devices with their start and end apart: 19, of which 7 were waited for; matrix products, arithmetic and copies ran while one was open for 0% of the time, Pallas kernels for 20%

profile of v2, /device:TPU:0, one launch (start us, length us, event | category | flops | bytes accessed | tf_op | source)
XLA Modules:
  0.0 56.4 jit_solution(14147228745947588520)
XLA Ops:
  0.0 2.9 %copy-done = bf16[640,5120]{1,0:T(8,128)(2,1)S(1)} copy-done((bf16[640,5120]{1,0:T(8,128)(2,1)S(1)}, bf16[640,5120]{1,0:T(8,128)(2,1)}, u32[]{:S(2)}) %copy-start) | copy-done | bytes 6553624
  2.9 0.9 %split_weights.1 = (bf16[640,2560]{1,0:T(8,128)(2,1)S(1)}, bf16[640,2560]{1,0:T(8,128)(2,1)S(1)}) custom-call(bf16[640,5120]{1,0:T(8,128)(2,1)S(1)} %copy-done), custom_call_target="tpu_custom_call" | custom-call | bytes 13107200 | tf_op jit(solution)/shard_map/split_weights/pallas_call | solution.py:163
  3.8 0.6 collective-permute-start.15
  4.3 2.6 %collective-permute-start = (bf16[160,640]{1,0:T(8,128)(2,1)S(1)}, bf16[160,640]{1,0:T(8,128)(2,1)S(1)}, u32[]{:S(2)}, u32[]{:S(2)}) collective-permute-start(bf16[160,640]{1,0:T(8,128)(2,1)S(1)} %copy-done.2), channel_id=1, source_target_pairs={{0,8},{8,16},{16,24},{24,28},{28,20},{20,12},{12,4},{4,0},{1,9},{9... | collective-permute-start | bytes 614408 | tf_op jit(solution)/shard_map/ppermute | solution.py:266
  7.0 2.0 %collective-permute-start.4 = (bf16[160,640]{1,0:T(8,128)(2,1)S(1)}, bf16[160,640]{1,0:T(8,128)(2,1)S(1)}, u32[]{:S(2)}, u32[]{:S(2)}) collective-permute-start(bf16[160,640]{1,0:T(8,128)(2,1)S(1)} %copy-done.2), channel_id=1, source_target_pairs={{8,0},{16,8},{24,16},{28,24},{20,28},{12,20},{4,12},{0,4},{9,1},{1... | collective-permute-start | bytes 614408 | tf_op jit(solution)/shard_map/ppermute | solution.py:269
  9.0 3.8 %collective-permute-done.refs_1_ = bf16[160,640]{1,0:T(8,128)(2,1)S(1)} collective-permute-done((bf16[160,640]{1,0:T(8,128)(2,1)S(1)}, bf16[160,640]{1,0:T(8,128)(2,1)S(1)}, u32[]{:S(2)}, u32[]{:S(2)}) %collective-permute-start) | collective-permute-done | bytes 204832 | tf_op jit(solution)/shard_map/ppermute | solution.py:266
  12.8 2.1 %collective-permute-start.1 = (bf16[160,640]{1,0:T(8,128)(2,1)S(1)}, bf16[160,640]{1,0:T(8,128)(2,1)S(1)}, u32[]{:S(2)}, u32[]{:S(2)}) collective-permute-start(bf16[160,640]{1,0:T(8,128)(2,1)S(1)} %collective-permute-done.refs_1_), channel_id=1, source_target_pairs={{0,8},{8,16},{16,24},{24,28},{28,20},{20,12},{12,4},{4,0},{1,9},{9... | collective-permute-start | bytes 614408 | tf_op jit(solution)/shard_map/ppermute | solution.py:266
  14.9 4.4 %collective-permute-done.4.refs_2_ = bf16[160,640]{1,0:T(8,128)(2,1)S(1)} collective-permute-done((bf16[160,640]{1,0:T(8,128)(2,1)S(1)}, bf16[160,640]{1,0:T(8,128)(2,1)S(1)}, u32[]{:S(2)}, u32[]{:S(2)}) %collective-permute-start.4) | collective-permute-done | bytes 204832 | tf_op jit(solution)/shard_map/ppermute | solution.py:269
  19.3 2.0 %collective-permute-start.8 = (bf16[160,640]{1,0:T(8,128)(2,1)S(1)}, bf16[160,640]{1,0:T(8,128)(2,1)S(1)}, u32[]{:S(2)}, u32[]{:S(2)}) collective-permute-start(bf16[160,640]{1,0:T(8,128)(2,1)S(1)} %collective-permute-done.7.refs_3_), channel_id=1, source_target_pairs={{0,8},{8,16},{16,24},{24,28},{28,20},{20,12},{12,4},{4,0},{1,9},{9... | collective-permute-start | bytes 614408 | tf_op jit(solution)/shard_map/ppermute | solution.py:268
  21.4 0.3 collective-permute-done.1.refs_1_
  21.6 2.1 %collective-permute-start.2 = (bf16[160,640]{1,0:T(8,128)(2,1)S(1)}, bf16[160,640]{1,0:T(8,128)(2,1)S(1)}, u32[]{:S(2)}, u32[]{:S(2)}) collective-permute-start(bf16[160,640]{1,0:T(8,128)(2,1)S(1)} %collective-permute-done.1.refs_1_), channel_id=1, source_target_pairs={{0,8},{8,16},{16,24},{24,28},{28,20},{20,12},{12,4},{4,0},{1,9},{9... | collective-permute-start | bytes 614408 | tf_op jit(solution)/shard_map/ppermute | solution.py:266
  23.7 4.4 %collective-permute-done.5.refs_2_ = bf16[160,640]{1,0:T(8,128)(2,1)S(1)} collective-permute-done((bf16[160,640]{1,0:T(8,128)(2,1)S(1)}, bf16[160,640]{1,0:T(8,128)(2,1)S(1)}, u32[]{:S(2)}, u32[]{:S(2)}) %collective-permute-start.5) | collective-permute-done | bytes 204832 | tf_op jit(solution)/shard_map/ppermute | solution.py:269
  28.1 2.0 %collective-permute-start.9 = (bf16[160,640]{1,0:T(8,128)(2,1)S(1)}, bf16[160,640]{1,0:T(8,128)(2,1)S(1)}, u32[]{:S(2)}, u32[]{:S(2)}) collective-permute-start(bf16[160,640]{1,0:T(8,128)(2,1)S(1)} %collective-permute-done.8.refs_3_), channel_id=1, source_target_pairs={{0,8},{8,16},{16,24},{24,28},{28,20},{20,12},{12,4},{4,0},{1,9},{9... | collective-permute-start | bytes 614408 | tf_op jit(solution)/shard_map/ppermute | solution.py:268
  30.1 0.7 %collective-permute-done.2.refs_1_ = bf16[160,640]{1,0:T(8,128)(2,1)S(1)} collective-permute-done((bf16[160,640]{1,0:T(8,128)(2,1)S(1)}, bf16[160,640]{1,0:T(8,128)(2,1)S(1)}, u32[]{:S(2)}, u32[]{:S(2)}) %collective-permute-start.2) | collective-permute-done | bytes 204832 | tf_op jit(solution)/shard_map/ppermute | solution.py:266
  30.8 2.1 %collective-permute-start.3 = (bf16[160,640]{1,0:T(8,128)(2,1)S(1)}, bf16[160,640]{1,0:T(8,128)(2,1)S(1)}, u32[]{:S(2)}, u32[]{:S(2)}) collective-permute-start(bf16[160,640]{1,0:T(8,128)(2,1)S(1)} %collective-permute-done.2.refs_1_), channel_id=1, source_target_pairs={{0,8},{8,16},{16,24},{24,28},{28,20},{20,12},{12,4},{4,0},{1,9},{9... | collective-permute-start | bytes 614408 | tf_op jit(solution)/shard_map/ppermute | solution.py:271
  33.0 0.8 %flash.4 = (f32[160,640]{1,0:T(8,128)S(1)}, f32[160,640]{1,0:T(8,128)S(1)}, f32[160,640]{1,0:T(8,128)S(1)}) custom-call(bf16[160,640]{1,0:T(8,128)(2,1)S(1)} %copy-done.1, bf16[160,640]{1,0:T(8,128)(2,1)S(1)} %copy-done.2, bf16[160,640]{1,0:T(8,128)(2,1)S(1)} %copy-done.3), custom_call_target="tpu_custom_call" | custom-call | flops 65536000 | bytes 3072000 | tf_op jit(solution)/shard_map/flash/pallas_call | solution.py:66
  33.8 1.9 %flash.5 = (f32[160,640]{1,0:T(8,128)S(1)}, f32[160,640]{1,0:T(8,128)S(1)}, f32[160,640]{1,0:T(8,128)S(1)}) custom-call(bf16[160,640]{1,0:T(8,128)(2,1)S(1)} %copy-done.1, bf16[160,640]{1,0:T(8,128)(2,1)S(1)} %collective-permute-done.refs_1_, bf16[160,640]{1,0:T(8,128)(2,1)S(1)} %collective-permute-done.4.refs_2_, ...), custom_call_target="tpu_custom_call" | custom-call | flops 131072000 | bytes 3481600 | tf_op jit(solution)/shard_map/flash/pallas_call | solution.py:66
  35.6 1.9 %flash.6 = (f32[160,640]{1,0:T(8,128)S(1)}, f32[160,640]{1,0:T(8,128)S(1)}, f32[160,640]{1,0:T(8,128)S(1)}) custom-call(bf16[160,640]{1,0:T(8,128)(2,1)S(1)} %copy-done.1, bf16[160,640]{1,0:T(8,128)(2,1)S(1)} %collective-permute-done.1.refs_1_, bf16[160,640]{1,0:T(8,128)(2,1)S(1)} %collective-permute-done.5.refs_2_, ...), custom_call_target="tpu_custom_call" | custom-call | flops 131072000 | bytes 3481600 | tf_op jit(solution)/shard_map/flash/pallas_call | solution.py:66
  37.5 1.9 %flash.7 = (f32[160,640]{1,0:T(8,128)S(1)}, f32[160,640]{1,0:T(8,128)S(1)}, f32[160,640]{1,0:T(8,128)S(1)}) custom-call(bf16[160,640]{1,0:T(8,128)(2,1)S(1)} %copy-done.1, bf16[160,640]{1,0:T(8,128)(2,1)S(1)} %collective-permute-done.2.refs_1_, bf16[160,640]{1,0:T(8,128)(2,1)S(1)} %collective-permute-done.6.refs_2_, ...), custom_call_target="tpu_custom_call" | custom-call | flops 131072000 | bytes 3481600 | tf_op jit(solution)/shard_map/flash/pallas_call | solution.py:66
  39.4 1.1 %last_scores.1 = (bf16[5,160,160]{2,1,0:T(8,128)(2,1)S(1)}, f32[160,640]{1,0:T(8,128)S(1)}, f32[160,640]{1,0:T(8,128)S(1)}) custom-call(bf16[160,640]{1,0:T(8,128)(2,1)S(1)} %copy-done.1, bf16[160,640]{1,0:T(8,128)(2,1)S(1)} %collective-permute-done.3.k_ref, f32[160,640]{1,0:T(8,128)S(1)} %get-tuple-element.31.acc_in, ...), custom_call_target="tpu_custom_call" | custom-call | flops 32768000 | bytes 2457600 | tf_op jit(solution)/shard_map/last_scores/pallas_call | solution.py:103
  40.8 0.5 project.8.refs_0_
  41.3 0.9 %collective-permute-done.14.a_ref = bf16[160,640]{1,0:T(8,128)(2,1)S(1)} collective-permute-done((bf16[160,640]{1,0:T(8,128)(2,1)S(1)}, bf16[160,640]{1,0:T(8,128)(2,1)S(1)}, u32[]{:S(2)}, u32[]{:S(2)}) %collective-permute-start.14) | collective-permute-done | bytes 204832 | tf_op jit(solution)/shard_map/ppermute | solution.py:275
  42.3 0.3 project.10
  42.6 2.0 %collective-permute-start.17 = (bf16[160,512]{1,0:T(8,128)(2,1)S(1)}, bf16[160,512]{1,0:T(8,128)(2,1)S(1)}, u32[]{:S(2)}, u32[]{:S(2)}) collective-permute-start(bf16[160,512]{1,0:T(8,128)(2,1)S(1)} %project.10), channel_id=1, source_target_pairs={{0,2},{1,3},{2,0},{3,1},{4,6},{5,7},{6,4},{7,5},{8,10},{9,11},{10,... | collective-permute-start | bytes 491528 | tf_op jit(solution)/shard_map/ppermute | solution.py:285
  44.6 0.3 project.9
  45.3 2.0 %collective-permute-start.18 = (bf16[160,256]{1,0:T(8,128)(2,1)S(1)}, bf16[160,256]{1,0:T(8,128)(2,1)S(1)}, u32[]{:S(2)}, u32[]{:S(2)}) collective-permute-start(bf16[160,256]{1,0:T(8,128)(2,1)S(1)} %project.11), channel_id=1, source_target_pairs={{0,2},{1,3},{2,0},{3,1},{4,6},{5,7},{6,4},{7,5},{8,10},{9,11},{10,... | collective-permute-start | bytes 245768 | tf_op jit(solution)/shard_map/ppermute | solution.py:285
  47.3 0.5 project.6.refs_0_
  47.8 0.5 project.7.refs_0_
  48.3 6.1 %collective-permute-done.18.refs_1_ = bf16[160,256]{1,0:T(8,128)(2,1)S(1)} collective-permute-done((bf16[160,256]{1,0:T(8,128)(2,1)S(1)}, bf16[160,256]{1,0:T(8,128)(2,1)S(1)}, u32[]{:S(2)}, u32[]{:S(2)}) %collective-permute-start.18) | collective-permute-done | bytes 81952 | tf_op jit(solution)/shard_map/ppermute | solution.py:285
  54.3 0.7 %finish.3.refs_2_ = bf16[160,1280]{1,0:T(8,128)(2,1)} custom-call(f32[160,1280]{1,0:T(8,128)S(1)} %project.7.refs_0_, bf16[160,256]{1,0:T(8,128)(2,1)S(1)} %collective-permute-done.18.refs_1_), custom_call_target="tpu_custom_call" | custom-call | flops 40960 | bytes 327680 | tf_op jit(solution)/shard_map/finish/pallas_call | solution.py:226
  55.0 0.7 %finish.4.refs_2_ = bf16[160,1280]{1,0:T(8,128)(2,1)} custom-call(f32[160,1280]{1,0:T(8,128)S(1)} %project.7.refs_0_, bf16[160,512]{1,0:T(8,128)(2,1)S(1)} %collective-permute-done.17.refs_1_, bf16[160,1280]{1,0:T(8,128)(2,1)} %finish.3.refs_2_), custom_call_target="tpu_custom_call", output_to_operand_aliasing={{}: (2, {})} | custom-call | flops 81920 | bytes 655360 | tf_op jit(solution)/shard_map/finish/pallas_call | solution.py:226
  55.7 0.7 %finish.5 = bf16[160,1280]{1,0:T(8,128)(2,1)} custom-call(f32[160,1280]{1,0:T(8,128)S(1)} %project.7.refs_0_, bf16[160,512]{1,0:T(8,128)(2,1)S(1)} %collective-permute-done.16.refs_1_, bf16[160,1280]{1,0:T(8,128)(2,1)} %finish.4.refs_2_), custom_call_target="tpu_custom_call", output_to_operand_aliasing={{}: (2, {})} | custom-call | flops 81920 | bytes 655360 | tf_op jit(solution)/shard_map/finish/pallas_call | solution.py:226
  (30 shorter events, 0.9 us)
Async XLA Ops:
  0.0 2.9 %copy-start = (bf16[640,5120]{1,0:T(8,128)(2,1)S(1)}, bf16[640,5120]{1,0:T(8,128)(2,1)}, u32[]{:S(2)}) copy-start(bf16[640,5120]{1,0:T(8,128)(2,1)} %w_ref.1) | copy-start | bytes 19660804
  2.9 1.5 %copy-start.2 = (bf16[160,640]{1,0:T(8,128)(2,1)S(1)}, bf16[160,640]{1,0:T(8,128)(2,1)}, u32[]{:S(2)}) copy-start(bf16[160,640]{1,0:T(8,128)(2,1)} %refs_1_.1) | copy-start | bytes 614404
  2.9 4.1 %copy-start.3 = (bf16[160,640]{1,0:T(8,128)(2,1)S(1)}, bf16[160,640]{1,0:T(8,128)(2,1)}, u32[]{:S(2)}) copy-start(bf16[160,640]{1,0:T(8,128)(2,1)} %refs_2_.1) | copy-start | bytes 614404
  2.9 30.1 %copy-start.1 = (bf16[160,640]{1,0:T(8,128)(2,1)S(1)}, bf16[160,640]{1,0:T(8,128)(2,1)}, u32[]{:S(2)}) copy-start(bf16[160,640]{1,0:T(8,128)(2,1)} %q_ref.1) | copy-start | bytes 614404
  3.8 38.5 %collective-permute-start.15 = (bf16[640,2560]{1,0:T(8,128)(2,1)S(1)}, bf16[640,2560]{1,0:T(8,128)(2,1)S(1)}, u32[]{:S(2)}, u32[]{:S(2)}) collective-permute-start(bf16[640,2560]{1,0:T(8,128)(2,1)S(1)} %get-tuple-element.37), channel_id=1, source_target_pairs={{0,1},{1,0},{2,3},{3,2},{4,5},{5,4},{6,7},{7,6},{8,9},{9,8},{10,11... | collective-permute-start | bytes 9830408 | tf_op jit(solution)/shard_map/ppermute | solution.py:261
  4.3 8.5 %collective-permute-start = (bf16[160,640]{1,0:T(8,128)(2,1)S(1)}, bf16[160,640]{1,0:T(8,128)(2,1)S(1)}, u32[]{:S(2)}, u32[]{:S(2)}) collective-permute-start(bf16[160,640]{1,0:T(8,128)(2,1)S(1)} %copy-done.2), channel_id=1, source_target_pairs={{0,8},{8,16},{16,24},{24,28},{28,20},{20,12},{12,4},{4,0},{1,9},{9... | collective-permute-start | bytes 614408 | tf_op jit(solution)/shard_map/ppermute | solution.py:266
  7.0 8.0 %collective-permute-start.10 = (bf16[160,640]{1,0:T(8,128)(2,1)S(1)}, bf16[160,640]{1,0:T(8,128)(2,1)S(1)}, u32[]{:S(2)}, u32[]{:S(2)}) collective-permute-start(bf16[160,640]{1,0:T(8,128)(2,1)S(1)} %copy-done.3), channel_id=1, source_target_pairs={{8,0},{16,8},{24,16},{28,24},{20,28},{12,20},{4,12},{0,4},{9,1},{1... | collective-permute-start | bytes 614408 | tf_op jit(solution)/shard_map/ppermute | solution.py:267
  7.0 12.3 %collective-permute-start.4 = (bf16[160,640]{1,0:T(8,128)(2,1)S(1)}, bf16[160,640]{1,0:T(8,128)(2,1)S(1)}, u32[]{:S(2)}, u32[]{:S(2)}) collective-permute-start(bf16[160,640]{1,0:T(8,128)(2,1)S(1)} %copy-done.2), channel_id=1, source_target_pairs={{8,0},{16,8},{24,16},{28,24},{20,28},{12,20},{4,12},{0,4},{9,1},{1... | collective-permute-start | bytes 614408 | tf_op jit(solution)/shard_map/ppermute | solution.py:269
  8.9 10.4 %collective-permute-start.7 = (bf16[160,640]{1,0:T(8,128)(2,1)S(1)}, bf16[160,640]{1,0:T(8,128)(2,1)S(1)}, u32[]{:S(2)}, u32[]{:S(2)}) collective-permute-start(bf16[160,640]{1,0:T(8,128)(2,1)S(1)} %copy-done.3), channel_id=1, source_target_pairs={{0,8},{8,16},{16,24},{24,28},{28,20},{20,12},{12,4},{4,0},{1,9},{9... | collective-permute-start | bytes 614408 | tf_op jit(solution)/shard_map/ppermute | solution.py:268
  12.8 8.8 %collective-permute-start.1 = (bf16[160,640]{1,0:T(8,128)(2,1)S(1)}, bf16[160,640]{1,0:T(8,128)(2,1)S(1)}, u32[]{:S(2)}, u32[]{:S(2)}) collective-permute-start(bf16[160,640]{1,0:T(8,128)(2,1)S(1)} %collective-permute-done.refs_1_), channel_id=1, source_target_pairs={{0,8},{8,16},{16,24},{24,28},{28,20},{20,12},{12,4},{4,0},{1,9},{9... | collective-permute-start | bytes 614408 | tf_op jit(solution)/shard_map/ppermute | solution.py:266
  14.9 8.8 %collective-permute-start.11 = (bf16[160,640]{1,0:T(8,128)(2,1)S(1)}, bf16[160,640]{1,0:T(8,128)(2,1)S(1)}, u32[]{:S(2)}, u32[]{:S(2)}) collective-permute-start(bf16[160,640]{1,0:T(8,128)(2,1)S(1)} %collective-permute-done.10.refs_4_), channel_id=1, source_target_pairs={{8,0},{16,8},{24,16},{28,24},{20,28},{12,20},{4,12},{0,4},{9,1},{1... | collective-permute-start | bytes 614408 | tf_op jit(solution)/shard_map/ppermute | solution.py:267
  19.3 8.8 %collective-permute-start.5 = (bf16[160,640]{1,0:T(8,128)(2,1)S(1)}, bf16[160,640]{1,0:T(8,128)(2,1)S(1)}, u32[]{:S(2)}, u32[]{:S(2)}) collective-permute-start(bf16[160,640]{1,0:T(8,128)(2,1)S(1)} %collective-permute-done.4.refs_2_), channel_id=1, source_target_pairs={{8,0},{16,8},{24,16},{28,24},{20,28},{12,20},{4,12},{0,4},{9,1},{1... | collective-permute-start | bytes 614408 | tf_op jit(solution)/shard_map/ppermute | solution.py:269
  19.3 8.8 %collective-permute-start.8 = (bf16[160,640]{1,0:T(8,128)(2,1)S(1)}, bf16[160,640]{1,0:T(8,128)(2,1)S(1)}, u32[]{:S(2)}, u32[]{:S(2)}) collective-permute-start(bf16[160,640]{1,0:T(8,128)(2,1)S(1)} %collective-permute-done.7.refs_3_), channel_id=1, source_target_pairs={{0,8},{8,16},{16,24},{24,28},{28,20},{20,12},{12,4},{4,0},{1,9},{9... | collective-permute-start | bytes 614408 | tf_op jit(solution)/shard_map/ppermute | solution.py:268
  21.6 9.2 %collective-permute-start.2 = (bf16[160,640]{1,0:T(8,128)(2,1)S(1)}, bf16[160,640]{1,0:T(8,128)(2,1)S(1)}, u32[]{:S(2)}, u32[]{:S(2)}) collective-permute-start(bf16[160,640]{1,0:T(8,128)(2,1)S(1)} %collective-permute-done.1.refs_1_), channel_id=1, source_target_pairs={{0,8},{8,16},{16,24},{24,28},{28,20},{20,12},{12,4},{4,0},{1,9},{9... | collective-permute-start | bytes 614408 | tf_op jit(solution)/shard_map/ppermute | solution.py:266
  23.7 9.3 %collective-permute-start.12 = (bf16[160,640]{1,0:T(8,128)(2,1)S(1)}, bf16[160,640]{1,0:T(8,128)(2,1)S(1)}, u32[]{:S(2)}, u32[]{:S(2)}) collective-permute-start(bf16[160,640]{1,0:T(8,128)(2,1)S(1)} %collective-permute-done.11.refs_4_), channel_id=1, source_target_pairs={{8,0},{16,8},{24,16},{28,24},{20,28},{12,20},{4,12},{0,4},{9,1},{1... | collective-permute-start | bytes 614408 | tf_op jit(solution)/shard_map/ppermute | solution.py:267
  28.1 9.4 %collective-permute-start.6 = (bf16[160,640]{1,0:T(8,128)(2,1)S(1)}, bf16[160,640]{1,0:T(8,128)(2,1)S(1)}, u32[]{:S(2)}, u32[]{:S(2)}) collective-permute-start(bf16[160,640]{1,0:T(8,128)(2,1)S(1)} %collective-permute-done.5.refs_2_), channel_id=1, source_target_pairs={{8,0},{16,8},{24,16},{28,24},{20,28},{12,20},{4,12},{0,4},{9,1},{1... | collective-permute-start | bytes 614408 | tf_op jit(solution)/shard_map/ppermute | solution.py:269
  28.1 9.4 %collective-permute-start.9 = (bf16[160,640]{1,0:T(8,128)(2,1)S(1)}, bf16[160,640]{1,0:T(8,128)(2,1)S(1)}, u32[]{:S(2)}, u32[]{:S(2)}) collective-permute-start(bf16[160,640]{1,0:T(8,128)(2,1)S(1)} %collective-permute-done.8.refs_3_), channel_id=1, source_target_pairs={{0,8},{8,16},{16,24},{24,28},{28,20},{20,12},{12,4},{4,0},{1,9},{9... | collective-permute-start | bytes 614408 | tf_op jit(solution)/shard_map/ppermute | solution.py:268
  30.8 8.5 %collective-permute-start.3 = (bf16[160,640]{1,0:T(8,128)(2,1)S(1)}, bf16[160,640]{1,0:T(8,128)(2,1)S(1)}, u32[]{:S(2)}, u32[]{:S(2)}) collective-permute-start(bf16[160,640]{1,0:T(8,128)(2,1)S(1)} %collective-permute-done.2.refs_1_), channel_id=1, source_target_pairs={{0,8},{8,16},{16,24},{24,28},{28,20},{20,12},{12,4},{4,0},{1,9},{9... | collective-permute-start | bytes 614408 | tf_op jit(solution)/shard_map/ppermute | solution.py:271
  33.0 7.5 %collective-permute-start.13 = (bf16[160,640]{1,0:T(8,128)(2,1)S(1)}, bf16[160,640]{1,0:T(8,128)(2,1)S(1)}, u32[]{:S(2)}, u32[]{:S(2)}) collective-permute-start(bf16[160,640]{1,0:T(8,128)(2,1)S(1)} %collective-permute-done.12.refs_4_), channel_id=1, source_target_pairs={{8,0},{16,8},{24,16},{28,24},{20,28},{12,20},{4,12},{0,4},{9,1},{1... | collective-permute-start | bytes 614408 | tf_op jit(solution)/shard_map/ppermute | solution.py:272
  40.7 1.5 %collective-permute-start.14 = (bf16[160,640]{1,0:T(8,128)(2,1)S(1)}, bf16[160,640]{1,0:T(8,128)(2,1)S(1)}, u32[]{:S(2)}, u32[]{:S(2)}) collective-permute-start(bf16[160,640]{1,0:T(8,128)(2,1)S(1)} %last_values.1.a_ref), channel_id=1, source_target_pairs={{0,1},{1,0},{2,3},{3,2},{4,5},{5,4},{6,7},{7,6},{8,9},{9,8},{10,11... | collective-permute-start | bytes 614408 | tf_op jit(solution)/shard_map/ppermute | solution.py:275
  42.6 12.4 %collective-permute-start.17 = (bf16[160,512]{1,0:T(8,128)(2,1)S(1)}, bf16[160,512]{1,0:T(8,128)(2,1)S(1)}, u32[]{:S(2)}, u32[]{:S(2)}) collective-permute-start(bf16[160,512]{1,0:T(8,128)(2,1)S(1)} %project.10), channel_id=1, source_target_pairs={{0,2},{1,3},{2,0},{3,1},{4,6},{5,7},{6,4},{7,5},{8,10},{9,11},{10,... | collective-permute-start | bytes 491528 | tf_op jit(solution)/shard_map/ppermute | solution.py:285
  44.9 10.8 %collective-permute-start.16 = (bf16[160,512]{1,0:T(8,128)(2,1)S(1)}, bf16[160,512]{1,0:T(8,128)(2,1)S(1)}, u32[]{:S(2)}, u32[]{:S(2)}) collective-permute-start(bf16[160,512]{1,0:T(8,128)(2,1)S(1)} %project.9), channel_id=1, source_target_pairs={{0,2},{1,3},{2,0},{3,1},{4,6},{5,7},{6,4},{7,5},{8,10},{9,11},{10,... | collective-permute-start | bytes 491528 | tf_op jit(solution)/shard_map/ppermute | solution.py:285
  45.3 9.1 %collective-permute-start.18 = (bf16[160,256]{1,0:T(8,128)(2,1)S(1)}, bf16[160,256]{1,0:T(8,128)(2,1)S(1)}, u32[]{:S(2)}, u32[]{:S(2)}) collective-permute-start(bf16[160,256]{1,0:T(8,128)(2,1)S(1)} %project.11), channel_id=1, source_target_pairs={{0,2},{1,3},{2,0},{3,1},{4,6},{5,7},{6,4},{7,5},{8,10},{9,11},{10,... | collective-permute-start | bytes 245768 | tf_op jit(solution)/shard_map/ppermute | solution.py:285

commit v3 on v2

--- a/solution.py
+++ b/solution.py
@@ -11,6 +11,7 @@
 
 HD = 128
 VM = pl.BlockSpec(memory_space=pltpu.VMEM)
+HBM = pl.BlockSpec(memory_space=pltpu.HBM)
 GRANT = 8 * 2**20
 PIECE = 512
 
@@ -29,25 +30,53 @@
         acc_in, top_in, total_in = rest[:3]
         rest = rest[3:]
     acc_ref, top_ref, total_ref = rest
+
+    def part(h):
+        return slice(h * HD, (h + 1) * HD)
+
+    def scores_of(h):
+        key = jnp.concatenate([ref[:, part(h)] for ref in k_refs], axis=0)
+        return score(q_ref[:, part(h)], key)
+
+    def weights_of(h, scores):
+        top = jnp.broadcast_to(jnp.max(scores, axis=1, keepdims=True), (rows, HD))
+        shrink = None
+        if not first:
+            old_top = top_in[:, part(h)]
+            top = jnp.maximum(top, old_top)
+            shrink = jnp.exp2(old_top - top)
+        expo = jnp.exp2(scores - spread(top, scores.shape[1]))
+        total = jnp.broadcast_to(jnp.sum(expo, axis=1, keepdims=True), (rows, HD))
+        if not first:
+            total = total + shrink * total_in[:, part(h)]
+        top_ref[:, part(h)] = top
+        total_ref[:, part(h)] = total
+        return expo.astype(jnp.bfloat16), shrink
+
+    def values_of(h, expo, shrink):
+        value = jnp.concatenate([ref[:, part(h)] for ref in v_refs], axis=0)
+        summed = jnp.dot(expo, value, preferred_element_type=jnp.float32)
+        if not first:
+            summed = summed + shrink * acc_in[:, part(h)]
+        acc_ref[:, part(h)] = summed
+
+    ahead = scores_of(0)
+    weights = None
     for h in range(heads):
-        cols = slice(h * HD, (h + 1) * HD)
-        key = jnp.concatenate([ref[:, cols] for ref in k_refs], axis=0)
-        value = jnp.concatenate([ref[:, cols] for ref in v_refs], axis=0)
-        scores = score(q_ref[:, cols], key)
-        top = jnp.broadcast_to(jnp.max(scores, axis=1, keepdims=True), (rows, HD))
-        if not first:
-            old_top = top_in[:, cols]
-            top = jnp.maximum(top, old_top)
-        expo = jnp.exp2(scores - top[:, :1])
-        total = jnp.broadcast_to(jnp.sum(expo, axis=1, keepdims=True), (rows, HD))
-        summed = jnp.dot(expo.astype(jnp.bfloat16), value, preferred_element_type=jnp.float32)
-        if not first:
-            shrink = jnp.exp2(old_top - top)
-            total = total + shrink * total_in[:, cols]
-            summed = summed + shrink * acc_in[:, cols]
-        acc_ref[:, cols] = summed
-        top_ref[:, cols] = top
-        total_ref[:, cols] = total
+        scores = ahead
+        if h + 1 < heads:
+            ahead = scores_of(h + 1)
+        made = weights_of(h, scores)
+        if weights is not None:
+            values_of(h - 1, *weights)
+        weights = made
+    values_of(heads - 1, *weights)
+
+
+def spread(value, count):
+    whole, rest = divmod(count, HD)
+    pieces = [value] * whole + ([value[:, :rest]] if rest else [])
+    return jnp.concatenate(pieces, axis=1)
 
 
 def score(query, key):
@@ -78,21 +107,63 @@
     )(*args)
 
 
+def first_flash_kernel(heads, q_hbm, k_hbm, v_hbm, acc, top, total, q_ref, k_ref, v_ref, sems):
+    pairs = ((q_hbm, q_ref), (k_hbm, k_ref), (v_hbm, v_ref))
+    copies = [pltpu.make_async_copy(a, b, sems.at[i]) for i, (a, b) in enumerate(pairs)]
+    for copy in copies:
+        copy.start()
+    for copy in copies:
+        copy.wait()
+    flash_kernel(heads, 1, True, q_ref, k_ref, v_ref, acc, top, total)
+
+
+def first_flash(query, keys, values):
+    rows, width = query.shape
+    heads = width // HD
+    wide = jax.ShapeDtypeStruct((rows, width), jnp.float32)
+    count = keys.shape[0]
+    *state, query = pl.pallas_call(
+        functools.partial(first_flash_kernel, heads),
+        out_shape=(wide, wide, wide, jax.ShapeDtypeStruct(query.shape, query.dtype)),
+        in_specs=[HBM] * 3,
+        out_specs=[VM] * 4,
+        scratch_shapes=[
+            pltpu.VMEM(keys.shape, keys.dtype),
+            pltpu.VMEM(values.shape, values.dtype),
+            pltpu.SemaphoreType.DMA((3,)),
+        ],
+        cost_estimate=pl.CostEstimate(
+            flops=4 * rows * count * width,
+            transcendentals=rows * count * heads,
+            bytes_accessed=20 * rows * width,
+        ),
+        compiler_params=params(),
+        name="first_flash",
+    )(*(pltpu.with_memory_space_constraint(a, pltpu.HBM) for a in (query, keys, values)))
+    return query, state
+
+
 def last_scores_kernel(heads, q_ref, k_ref, acc_in, top_in, total_in, expo_ref, acc_ref, norm_ref):
     rows = q_ref.shape[0]
+
+    def part(h):
+        return slice(h * HD, (h + 1) * HD)
+
+    ahead = score(q_ref[:, part(0)], k_ref[:, part(0)])
     for h in range(heads):
-        cols = slice(h * HD, (h + 1) * HD)
-        scores = score(q_ref[:, cols], k_ref[:, cols])
-        old_top = top_in[:, cols]
+        scores = ahead
+        if h + 1 < heads:
+            ahead = score(q_ref[:, part(h + 1)], k_ref[:, part(h + 1)])
+        old_top = top_in[:, part(h)]
         top = jnp.broadcast_to(jnp.max(scores, axis=1, keepdims=True), (rows, HD))
         top = jnp.maximum(top, old_top)
-        expo = jnp.exp2(scores - top[:, :1])
+        expo = jnp.exp2(scores - spread(top, scores.shape[1]))
         total = jnp.broadcast_to(jnp.sum(expo, axis=1, keepdims=True), (rows, HD))
         shrink = jnp.exp2(old_top - top)
-        norm = jnp.exp2(-jnp.log2(total + shrink * total_in[:, cols]))
+        norm = pl.reciprocal(total + shrink * total_in[:, part(h)])
         expo_ref[h] = expo.astype(jnp.bfloat16)
-        acc_ref[:, cols] = acc_in[:, cols] * (shrink * norm)
-        norm_ref[:, cols] = norm
+        acc_ref[:, part(h)] = acc_in[:, part(h)] * (shrink * norm)
+        norm_ref[:, part(h)] = norm
 
 
 def last_scores(query, keys, state):
@@ -115,63 +186,63 @@
     )(query, keys, *state)
 
 
-def last_values_kernel(heads, expo_ref, v_ref, acc_ref, norm_ref, out_ref):
+def last_values_kernel(heads, expo_ref, upper_ref, lower_ref, acc_ref, norm_ref, out_ref):
     for h in range(heads):
         cols = slice(h * HD, (h + 1) * HD)
-        summed = jnp.dot(expo_ref[h], v_ref[:, cols], preferred_element_type=jnp.float32)
+        value = jnp.concatenate([upper_ref[:, cols], lower_ref[:, cols]], axis=0)
+        summed = jnp.dot(expo_ref[h], value, preferred_element_type=jnp.float32)
         out_ref[:, cols] = (acc_ref[:, cols] + summed * norm_ref[:, cols]).astype(out_ref.dtype)
 
 
-def last_values(expo, values, acc, norm):
+def last_values(expo, upper, lower, acc, norm):
     heads, rows, count = expo.shape
     width = heads * HD
     return pl.pallas_call(
         functools.partial(last_values_kernel, heads),
         out_shape=jax.ShapeDtypeStruct((rows, width), jnp.bfloat16),
-        in_specs=[VM] * 4,
+        in_specs=[VM] * 5,
         out_specs=VM,
         cost_estimate=pl.CostEstimate(
             flops=2 * rows * count * width, transcendentals=0, bytes_accessed=14 * rows * width
         ),
         compiler_params=params(),
         name="last_values",
-    )(expo, values, acc, norm)
-
-
-def weights_kernel(chips, columns, w_ref, mine_ref, other_ref, sems):
+    )(expo, upper, lower, acc, norm)
+
+
+def columns_kernel(chips, columns, partner, w_ref, out_ref, sems):
     place = lax.axis_index("head")
+    core = 1 - place % 2 if partner else place % 2
     copies = []
     for p in range(chips):
         target = lax.rem(place // 2 + p + 1, chips)
-        for side, out in enumerate((mine_ref, other_ref)):
-            core = place % 2 if side == 0 else 1 - place % 2
-            start = pl.multiple_of((2 * target + core) * columns, HD)
-            copy = pltpu.make_async_copy(
+        start = pl.multiple_of((2 * target + core) * columns, HD)
+        copies.append(
+            pltpu.make_async_copy(
                 w_ref.at[:, pl.ds(start, columns)],
-                out.at[:, pl.ds(p * columns, columns)],
-                sems.at[2 * p + side],
+                out_ref.at[:, pl.ds(p * columns, columns)],
+                sems.at[p],
             )
-            copy.start()
-            copies.append(copy)
+        )
+        copies[-1].start()
     for copy in copies:
         copy.wait()
 
 
-def split_weights(weight, chips, columns):
+def weight_columns(weight, chips, columns, partner):
     depth = weight.shape[0]
-    half = jax.ShapeDtypeStruct((depth, chips * columns), weight.dtype)
-    return pl.pallas_call(
-        functools.partial(weights_kernel, chips, columns),
-        out_shape=(half, half),
-        in_specs=[pl.BlockSpec(memory_space=pl.ANY)],
-        out_specs=(VM, VM),
-        scratch_shapes=[pltpu.SemaphoreType.DMA((2 * chips,))],
-        cost_estimate=pl.CostEstimate(
-            flops=0, transcendentals=0, bytes_accessed=8 * depth * chips * columns
-        ),
-        compiler_params=pltpu.CompilerParams(vmem_limit_bytes=2 * GRANT),
-        name="split_weights",
-    )(weight)
+    return pl.pallas_call(
+        functools.partial(columns_kernel, chips, columns, partner),
+        out_shape=jax.ShapeDtypeStruct((depth, chips * columns), weight.dtype),
+        in_specs=[HBM],
+        out_specs=VM,
+        scratch_shapes=[pltpu.SemaphoreType.DMA((chips,))],
+        cost_estimate=pl.CostEstimate(
+            flops=0, transcendentals=0, bytes_accessed=4 * depth * chips * columns
+        ),
+        compiler_params=params(),
+        name="weight_columns",
+    )(pltpu.with_memory_space_constraint(weight, pltpu.HBM))
 
 
 def project_kernel(first, tile, skip, a_ref, w_ref, *refs):
@@ -250,6 +321,7 @@
 
 
 def on_device(n_seq, n_head, queries, keys, values, out_weight):
+    rows = queries.shape[0]
     ahead, back = ring_pairs(n_seq)
     columns = out_weight.shape[1] // n_head
     chips = n_head // 2
@@ -257,9 +329,10 @@
     pieces = column_pieces(columns)
     steps = n_seq // 2
 
-    w_mine, w_give = split_weights(out_weight, chips, columns)
+    w_give = weight_columns(out_weight, chips, columns, True)
+    w_mine = weight_columns(out_weight, chips, columns, False)
     w_partner = lax.ppermute(w_give, "head", swap)
-    state = flash(queries, [keys], [values], ())
+    queries, state = first_flash(queries, keys, values)
     kf = kb = keys
     vf = vb = values
     for _ in range(1, steps):
@@ -269,9 +342,11 @@
         kb = lax.ppermute(kb, "seq", back)
         state = flash(queries, [kf, kb], [vf, vb], state)
     kf = lax.ppermute(kf, "seq", ahead)
-    vb = lax.ppermute(vb, "seq", back)
+    upper = rows * 4 // 5 // 16 * 16
+    v_upper = lax.ppermute(vb[:upper], "seq", back)
+    v_lower = lax.ppermute(vf[upper:], "seq", ahead)
     expo, acc, norm = last_scores(queries, kf, state)
-    attended = last_values(expo, vb, acc, norm)
+    attended = last_values(expo, v_upper, v_lower, acc, norm)
     partner = lax.ppermute(attended, "head", swap)
 
     away = (chips - 1) * columns

time: 56.6 us -> 57.1 us (level)
  local copies, waits for them, and re-layouts: 2.87 us -> 0.03 us
  starting transfers between devices: 19.8 us -> 21.6 us
  waiting for transfers between devices: 20.6 us -> 21.9 us
    ppermute x3, waiting for transfers between devices: 8.75 us -> 0.01 us  [on_device(): kb = lax.ppermute(kb, 'seq', back)]
    ppermute x3, waiting for transfers between devices: 0.01 us -> 6.8 us  [on_device(): vf = lax.ppermute(vf, 'seq', ahead)]
    pallas_call x1 -> x3, Pallas kernels: 0.91 us -> 5.68 us  [the longest x2 3.96 us: weight_columns(): pl.pallas_call(functools.partial(columns_kernel, chips, columns, partner)...]
    pallas_call x4 -> x3, Pallas kernels: 6.36 us -> 2.41 us  [flash(): pl.pallas_call(functools.partial(flash_kernel, heads, blocks, not state),...]
    ppermute x4, waiting for transfers between devices: 4.82 us -> 8.41 us  [on_device(): kf = lax.ppermute(kf, 'seq', ahead)]
    unnamed x8 -> x4, local copies, waits for them, and re-layouts: 2.87 us -> 0.01 us
    ppermute x0 -> x2, starting transfers between devices: none -> 2.14 us  [the longest x1 2.08 us: on_device(): v_lower = lax.ppermute(vf[upper:], 'seq', ahead)]
    ppermute x3, starting transfers between devices: 4.11 us -> 6.17 us  [on_device(): vf = lax.ppermute(vf, 'seq', ahead)]
  transfers between devices with their start and end apart: 19 -> 20, of which waited for: 7 -> 7; matrix products, arithmetic and copies ran while one was open for 0% -> 0% of each run, Pallas kernels for 20% -> 18%
where the time goes in v3:
time: 57.1 us; the launch traced here: 57 us
  waiting for transfers between devices  21.9 us (38%)
  starting transfers between devices  21.6 us (38%)
  Pallas kernels  13.3 us (23%)
    ppermute x4, starting transfers between devices, on_device(): kf = lax.ppermute(kf, 'seq', ahead)  8.87 us
    ppermute x4, waiting for transfers between devices, on_device(): kf = lax.ppermute(kf, 'seq', ahead)  8.41 us
    ppermute x3, waiting for transfers between devices, on_device(): vf = lax.ppermute(vf, 'seq', ahead)  6.8 us
    ppermute x3, waiting for transfers between devices, on_device(): arrived[index].append(lax.ppermute(given, 'head', pairs))  6.66 us
    ppermute x3, starting transfers between devices, on_device(): vf = lax.ppermute(vf, 'seq', ahead)  6.17 us
    pallas_call x2, Pallas kernels, weight_columns(): pl.pallas_call(functools.partial(columns_kernel, chips, columns, partner)...  3.96 us
    ppermute x3, starting transfers between devices, on_device(): arrived[index].append(lax.ppermute(given, 'head', pairs))  3.73 us
    pallas_call x3, Pallas kernels, flash(): pl.pallas_call(functools.partial(flash_kernel, heads, blocks, not state),...  2.41 us
  transfers between devices with their start and end apart: 20, of which 7 were waited for; matrix products, arithmetic and copies ran while one was open for 0% of the time, Pallas kernels for 18%

profile of v3, /device:TPU:0, one launch (start us, length us, event | category | flops | bytes accessed | tf_op | source)
XLA Modules:
  0.0 57.0 jit_solution(14446693177463884915)
XLA Ops:
  0.0 2.0 %weight_columns.2 = bf16[640,2560]{1,0:T(8,128)(2,1)S(1)} custom-call(bf16[640,5120]{1,0:T(8,128)(2,1)} %w_ref.3), custom_call_target="tpu_custom_call" | custom-call | bytes 6553600 | tf_op jit(solution)/shard_map/weight_columns/pallas_call | solution.py:234
  2.0 0.6 collective-permute-start.16
  2.6 2.6 %collective-permute-start = (bf16[160,640]{1,0:T(8,128)(2,1)S(1)}, bf16[160,640]{1,0:T(8,128)(2,1)S(1)}, u32[]{:S(2)}, u32[]{:S(2)}) collective-permute-start(bf16[160,640]{1,0:T(8,128)(2,1)S(1)} %copy-done), channel_id=1, source_target_pairs={{0,8},{8,16},{16,24},{24,28},{28,20},{20,12},{12,4},{4,0},{1,9},{9... | collective-permute-start | bytes 614408 | tf_op jit(solution)/shard_map/ppermute | solution.py:339
  5.2 2.0 %collective-permute-start.7 = (bf16[160,640]{1,0:T(8,128)(2,1)S(1)}, bf16[160,640]{1,0:T(8,128)(2,1)S(1)}, u32[]{:S(2)}, u32[]{:S(2)}) collective-permute-start(bf16[160,640]{1,0:T(8,128)(2,1)S(1)} %copy-done.1), channel_id=1, source_target_pairs={{0,8},{8,16},{16,24},{24,28},{28,20},{20,12},{12,4},{4,0},{1,9},{9... | collective-permute-start | bytes 614408 | tf_op jit(solution)/shard_map/ppermute | solution.py:341
  7.2 3.8 %collective-permute-done.refs_1_ = bf16[160,640]{1,0:T(8,128)(2,1)S(1)} collective-permute-done((bf16[160,640]{1,0:T(8,128)(2,1)S(1)}, bf16[160,640]{1,0:T(8,128)(2,1)S(1)}, u32[]{:S(2)}, u32[]{:S(2)}) %collective-permute-start) | collective-permute-done | bytes 204832 | tf_op jit(solution)/shard_map/ppermute | solution.py:339
  11.1 2.1 %collective-permute-start.1 = (bf16[160,640]{1,0:T(8,128)(2,1)S(1)}, bf16[160,640]{1,0:T(8,128)(2,1)S(1)}, u32[]{:S(2)}, u32[]{:S(2)}) collective-permute-start(bf16[160,640]{1,0:T(8,128)(2,1)S(1)} %collective-permute-done.refs_1_), channel_id=1, source_target_pairs={{0,8},{8,16},{16,24},{24,28},{28,20},{20,12},{12,4},{4,0},{1,9},{9... | collective-permute-start | bytes 614408 | tf_op jit(solution)/shard_map/ppermute | solution.py:339
  13.2 2.3 %collective-permute-done.7.refs_3_ = bf16[160,640]{1,0:T(8,128)(2,1)S(1)} collective-permute-done((bf16[160,640]{1,0:T(8,128)(2,1)S(1)}, bf16[160,640]{1,0:T(8,128)(2,1)S(1)}, u32[]{:S(2)}, u32[]{:S(2)}) %collective-permute-start.7) | collective-permute-done | bytes 204832 | tf_op jit(solution)/shard_map/ppermute | solution.py:341
  15.5 2.1 %collective-permute-start.8 = (bf16[160,640]{1,0:T(8,128)(2,1)S(1)}, bf16[160,640]{1,0:T(8,128)(2,1)S(1)}, u32[]{:S(2)}, u32[]{:S(2)}) collective-permute-start(bf16[160,640]{1,0:T(8,128)(2,1)S(1)} %collective-permute-done.7.refs_3_), channel_id=1, source_target_pairs={{0,8},{8,16},{16,24},{24,28},{28,20},{20,12},{12,4},{4,0},{1,9},{9... | collective-permute-start | bytes 614408 | tf_op jit(solution)/shard_map/ppermute | solution.py:341
  17.6 2.3 %collective-permute-done.1.refs_1_ = bf16[160,640]{1,0:T(8,128)(2,1)S(1)} collective-permute-done((bf16[160,640]{1,0:T(8,128)(2,1)S(1)}, bf16[160,640]{1,0:T(8,128)(2,1)S(1)}, u32[]{:S(2)}, u32[]{:S(2)}) %collective-permute-start.1) | collective-permute-done | bytes 204832 | tf_op jit(solution)/shard_map/ppermute | solution.py:339
  19.9 2.1 %collective-permute-start.2 = (bf16[160,640]{1,0:T(8,128)(2,1)S(1)}, bf16[160,640]{1,0:T(8,128)(2,1)S(1)}, u32[]{:S(2)}, u32[]{:S(2)}) collective-permute-start(bf16[160,640]{1,0:T(8,128)(2,1)S(1)} %collective-permute-done.1.refs_1_), channel_id=1, source_target_pairs={{0,8},{8,16},{16,24},{24,28},{28,20},{20,12},{12,4},{4,0},{1,9},{9... | collective-permute-start | bytes 614408 | tf_op jit(solution)/shard_map/ppermute | solution.py:339
  22.0 2.3 %collective-permute-done.8.refs_3_ = bf16[160,640]{1,0:T(8,128)(2,1)S(1)} collective-permute-done((bf16[160,640]{1,0:T(8,128)(2,1)S(1)}, bf16[160,640]{1,0:T(8,128)(2,1)S(1)}, u32[]{:S(2)}, u32[]{:S(2)}) %collective-permute-start.8) | collective-permute-done | bytes 204832 | tf_op jit(solution)/shard_map/ppermute | solution.py:341
  24.2 2.1 %collective-permute-start.9 = (bf16[160,640]{1,0:T(8,128)(2,1)S(1)}, bf16[160,640]{1,0:T(8,128)(2,1)S(1)}, u32[]{:S(2)}, u32[]{:S(2)}) collective-permute-start(bf16[160,640]{1,0:T(8,128)(2,1)S(1)} %collective-permute-done.8.refs_3_), channel_id=1, source_target_pairs={{0,8},{8,16},{16,24},{24,28},{28,20},{20,12},{12,4},{4,0},{1,9},{9... | collective-permute-start | bytes 614408 | tf_op jit(solution)/shard_map/ppermute | solution.py:341
  26.3 2.3 %collective-permute-done.2.refs_1_ = bf16[160,640]{1,0:T(8,128)(2,1)S(1)} collective-permute-done((bf16[160,640]{1,0:T(8,128)(2,1)S(1)}, bf16[160,640]{1,0:T(8,128)(2,1)S(1)}, u32[]{:S(2)}, u32[]{:S(2)}) %collective-permute-start.2) | collective-permute-done | bytes 204832 | tf_op jit(solution)/shard_map/ppermute | solution.py:339
  28.6 2.1 %collective-permute-start.3 = (bf16[160,640]{1,0:T(8,128)(2,1)S(1)}, bf16[160,640]{1,0:T(8,128)(2,1)S(1)}, u32[]{:S(2)}, u32[]{:S(2)}) collective-permute-start(bf16[160,640]{1,0:T(8,128)(2,1)S(1)} %collective-permute-done.2.refs_1_), channel_id=1, source_target_pairs={{0,8},{8,16},{16,24},{24,28},{28,20},{20,12},{12,4},{4,0},{1,9},{9... | collective-permute-start | bytes 614408 | tf_op jit(solution)/shard_map/ppermute | solution.py:344
  30.8 2.2 %collective-permute-done.9.refs_3_ = bf16[160,640]{1,0:T(8,128)(2,1)S(1)} collective-permute-done((bf16[160,640]{1,0:T(8,128)(2,1)S(1)}, bf16[160,640]{1,0:T(8,128)(2,1)S(1)}, u32[]{:S(2)}, u32[]{:S(2)}) %collective-permute-start.9) | collective-permute-done | bytes 204832 | tf_op jit(solution)/shard_map/ppermute | solution.py:341
  33.0 2.1 %collective-permute-start.14 = (bf16[32,640]{1,0:T(8,128)(2,1)S(1)}, bf16[32,640]{1,0:T(8,128)(2,1)S(1)}, u32[]{:S(2)}, u32[]{:S(2)}) collective-permute-start(bf16[32,640]{1,0:T(8,128)(2,1)S(1)} %slice.9), channel_id=1, source_target_pairs={{0,8},{8,16},{16,24},{24,28},{28,20},{20,12},{12,4},{4,0},{1,9},{9... | collective-permute-start | bytes 122888 | tf_op jit(solution)/shard_map/ppermute | solution.py:347
  35.1 1.7 %first_flash.1 = (f32[160,640]{1,0:T(8,128)S(1)}, f32[160,640]{1,0:T(8,128)S(1)}, f32[160,640]{1,0:T(8,128)S(1)}, bf16[160,640]{1,0:T(8,128)(2,1)S(1)}) custom-call(bf16[160,640]{1,0:T(8,128)(2,1)} %q_hbm.1, bf16[160,640]{1,0:T(8,128)(2,1)} %k_hbm.1, bf16[160,640]{1,0:T(8,128)(2,1)} %v_hbm.1), custom_call_target="tpu_custom_call" | custom-call | flops 65536000 | bytes 2048000 | tf_op jit(solution)/shard_map/first_flash/pallas_call | solution.py:125
  36.8 0.8 %flash.3 = (f32[160,640]{1,0:T(8,128)S(1)}, f32[160,640]{1,0:T(8,128)S(1)}, f32[160,640]{1,0:T(8,128)S(1)}) custom-call(bf16[160,640]{1,0:T(8,128)(2,1)S(1)} %get-tuple-element.21.refs_0_.q_ref, bf16[160,640]{1,0:T(8,128)(2,1)S(1)} %collective-permute-done.refs_1_, bf16[160,640]{1,0:T(8,128)(2,1)S(1)} %collective-permute-done.4.refs_2_, ...), custom_call_target="tpu_custom_call" | custom-call | flops 131072000 | bytes 3481600 | tf_op jit(solution)/shard_map/flash/pallas_call | solution.py:95
  37.6 0.8 %flash.4 = (f32[160,640]{1,0:T(8,128)S(1)}, f32[160,640]{1,0:T(8,128)S(1)}, f32[160,640]{1,0:T(8,128)S(1)}) custom-call(bf16[160,640]{1,0:T(8,128)(2,1)S(1)} %get-tuple-element.21.refs_0_.q_ref, bf16[160,640]{1,0:T(8,128)(2,1)S(1)} %collective-permute-done.1.refs_1_, bf16[160,640]{1,0:T(8,128)(2,1)S(1)} %collective-permute-done.5.refs_2_, ...), custom_call_target="tpu_custom_call" | custom-call | flops 131072000 | bytes 3481600 | tf_op jit(solution)/shard_map/flash/pallas_call | solution.py:95
  38.5 0.8 %flash.5 = (f32[160,640]{1,0:T(8,128)S(1)}, f32[160,640]{1,0:T(8,128)S(1)}, f32[160,640]{1,0:T(8,128)S(1)}) custom-call(bf16[160,640]{1,0:T(8,128)(2,1)S(1)} %get-tuple-element.21.refs_0_.q_ref, bf16[160,640]{1,0:T(8,128)(2,1)S(1)} %collective-permute-done.2.refs_1_, bf16[160,640]{1,0:T(8,128)(2,1)S(1)} %collective-permute-done.6.refs_2_, ...), custom_call_target="tpu_custom_call" | custom-call | flops 131072000 | bytes 3481600 | tf_op jit(solution)/shard_map/flash/pallas_call | solution.py:95
  39.3 0.6 %last_scores.1 = (bf16[5,160,160]{2,1,0:T(8,128)(2,1)S(1)}, f32[160,640]{1,0:T(8,128)S(1)}, f32[160,640]{1,0:T(8,128)S(1)}) custom-call(bf16[160,640]{1,0:T(8,128)(2,1)S(1)} %get-tuple-element.21.refs_0_.q_ref, bf16[160,640]{1,0:T(8,128)(2,1)S(1)} %collective-permute-done.3.k_ref, f32[160,640]{1,0:T(8,128)S(1)} %get-tuple-element.31.acc_in, ...), custom_call_target="tpu_custom_call" | custom-call | flops 32768000 | bytes 2457600 | tf_op jit(solution)/shard_map/last_scores/pallas_call | solution.py:174
  40.2 2.0 %weight_columns.3.w_ref = bf16[640,2560]{1,0:T(8,128)(2,1)S(1)} custom-call(bf16[640,5120]{1,0:T(8,128)(2,1)} %w_ref.3), custom_call_target="tpu_custom_call" | custom-call | bytes 6553600 | tf_op jit(solution)/shard_map/weight_columns/pallas_call | solution.py:234
  42.2 0.5 project.8.refs_0_
  43.0 1.6 %collective-permute-start.18 = (bf16[160,512]{1,0:T(8,128)(2,1)S(1)}, bf16[160,512]{1,0:T(8,128)(2,1)S(1)}, u32[]{:S(2)}, u32[]{:S(2)}) collective-permute-start(bf16[160,512]{1,0:T(8,128)(2,1)S(1)} %project.10), channel_id=1, source_target_pairs={{0,2},{1,3},{2,0},{3,1},{4,6},{5,7},{6,4},{7,5},{8,10},{9,11},{10,... | collective-permute-start | bytes 491528 | tf_op jit(solution)/shard_map/ppermute | solution.py:360
  44.9 0.6 %collective-permute-start.17 = (bf16[160,512]{1,0:T(8,128)(2,1)S(1)}, bf16[160,512]{1,0:T(8,128)(2,1)S(1)}, u32[]{:S(2)}, u32[]{:S(2)}) collective-permute-start(bf16[160,512]{1,0:T(8,128)(2,1)S(1)} %project.9), channel_id=1, source_target_pairs={{0,2},{1,3},{2,0},{3,1},{4,6},{5,7},{6,4},{7,5},{8,10},{9,11},{10,... | collective-permute-start | bytes 491528 | tf_op jit(solution)/shard_map/ppermute | solution.py:360
  45.7 1.6 %collective-permute-start.19 = (bf16[160,256]{1,0:T(8,128)(2,1)S(1)}, bf16[160,256]{1,0:T(8,128)(2,1)S(1)}, u32[]{:S(2)}, u32[]{:S(2)}) collective-permute-start(bf16[160,256]{1,0:T(8,128)(2,1)S(1)} %project.11), channel_id=1, source_target_pairs={{0,2},{1,3},{2,0},{3,1},{4,6},{5,7},{6,4},{7,5},{8,10},{9,11},{10,... | collective-permute-start | bytes 245768 | tf_op jit(solution)/shard_map/ppermute | solution.py:360
  47.3 0.5 project.6.refs_0_
  47.8 0.5 project.7.refs_0_
  48.3 6.7 %collective-permute-done.19.refs_1_ = bf16[160,256]{1,0:T(8,128)(2,1)S(1)} collective-permute-done((bf16[160,256]{1,0:T(8,128)(2,1)S(1)}, bf16[160,256]{1,0:T(8,128)(2,1)S(1)}, u32[]{:S(2)}, u32[]{:S(2)}) %collective-permute-start.19) | collective-permute-done | bytes 81952 | tf_op jit(solution)/shard_map/ppermute | solution.py:360
  54.9 0.7 %finish.3.refs_2_ = bf16[160,1280]{1,0:T(8,128)(2,1)} custom-call(f32[160,1280]{1,0:T(8,128)S(1)} %project.7.refs_0_, bf16[160,256]{1,0:T(8,128)(2,1)S(1)} %collective-permute-done.19.refs_1_), custom_call_target="tpu_custom_call" | custom-call | flops 40960 | bytes 327680 | tf_op jit(solution)/shard_map/finish/pallas_call | solution.py:297
  55.6 0.7 %finish.4.refs_2_ = bf16[160,1280]{1,0:T(8,128)(2,1)} custom-call(f32[160,1280]{1,0:T(8,128)S(1)} %project.7.refs_0_, bf16[160,512]{1,0:T(8,128)(2,1)S(1)} %collective-permute-done.18.refs_1_, bf16[160,1280]{1,0:T(8,128)(2,1)} %finish.3.refs_2_), custom_call_target="tpu_custom_call", output_to_operand_aliasing={{}: (2, {})} | custom-call | flops 81920 | bytes 655360 | tf_op jit(solution)/shard_map/finish/pallas_call | solution.py:297
  56.3 0.7 %finish.5 = bf16[160,1280]{1,0:T(8,128)(2,1)} custom-call(f32[160,1280]{1,0:T(8,128)S(1)} %project.7.refs_0_, bf16[160,512]{1,0:T(8,128)(2,1)S(1)} %collective-permute-done.17.refs_1_, bf16[160,1280]{1,0:T(8,128)(2,1)} %finish.4.refs_2_), custom_call_target="tpu_custom_call", output_to_operand_aliasing={{}: (2, {})} | custom-call | flops 81920 | bytes 655360 | tf_op jit(solution)/shard_map/finish/pallas_call | solution.py:297
  (31 shorter events, 1.4 us)
Async XLA Ops:
  0.0 2.6 %copy-start = (bf16[160,640]{1,0:T(8,128)(2,1)S(1)}, bf16[160,640]{1,0:T(8,128)(2,1)}, u32[]{:S(2)}) copy-start(bf16[160,640]{1,0:T(8,128)(2,1)} %k_hbm.1) | copy-start | bytes 614404
  0.0 5.2 %copy-start.1 = (bf16[160,640]{1,0:T(8,128)(2,1)S(1)}, bf16[160,640]{1,0:T(8,128)(2,1)}, u32[]{:S(2)}) copy-start(bf16[160,640]{1,0:T(8,128)(2,1)} %v_hbm.1) | copy-start | bytes 614404
  2.0 40.7 %collective-permute-start.16 = (bf16[640,2560]{1,0:T(8,128)(2,1)S(1)}, bf16[640,2560]{1,0:T(8,128)(2,1)S(1)}, u32[]{:S(2)}, u32[]{:S(2)}) collective-permute-start(bf16[640,2560]{1,0:T(8,128)(2,1)S(1)} %weight_columns.2), channel_id=1, source_target_pairs={{0,1},{1,0},{2,3},{3,2},{4,5},{5,4},{6,7},{7,6},{8,9},{9,8},{10,11... | collective-permute-start | bytes 9830408 | tf_op jit(solution)/shard_map/ppermute | solution.py:334
  2.6 8.5 %collective-permute-start = (bf16[160,640]{1,0:T(8,128)(2,1)S(1)}, bf16[160,640]{1,0:T(8,128)(2,1)S(1)}, u32[]{:S(2)}, u32[]{:S(2)}) collective-permute-start(bf16[160,640]{1,0:T(8,128)(2,1)S(1)} %copy-done), channel_id=1, source_target_pairs={{0,8},{8,16},{16,24},{24,28},{28,20},{20,12},{12,4},{4,0},{1,9},{9... | collective-permute-start | bytes 614408 | tf_op jit(solution)/shard_map/ppermute | solution.py:339
  5.2 8.0 %collective-permute-start.10 = (bf16[160,640]{1,0:T(8,128)(2,1)S(1)}, bf16[160,640]{1,0:T(8,128)(2,1)S(1)}, u32[]{:S(2)}, u32[]{:S(2)}) collective-permute-start(bf16[160,640]{1,0:T(8,128)(2,1)S(1)} %copy-done.1), channel_id=1, source_target_pairs={{8,0},{16,8},{24,16},{28,24},{20,28},{12,20},{4,12},{0,4},{9,1},{1... | collective-permute-start | bytes 614408 | tf_op jit(solution)/shard_map/ppermute | solution.py:340
  5.2 10.2 %collective-permute-start.7 = (bf16[160,640]{1,0:T(8,128)(2,1)S(1)}, bf16[160,640]{1,0:T(8,128)(2,1)S(1)}, u32[]{:S(2)}, u32[]{:S(2)}) collective-permute-start(bf16[160,640]{1,0:T(8,128)(2,1)S(1)} %copy-done.1), channel_id=1, source_target_pairs={{0,8},{8,16},{16,24},{24,28},{28,20},{20,12},{12,4},{4,0},{1,9},{9... | collective-permute-start | bytes 614408 | tf_op jit(solution)/shard_map/ppermute | solution.py:341
  7.2 10.3 %collective-permute-start.4 = (bf16[160,640]{1,0:T(8,128)(2,1)S(1)}, bf16[160,640]{1,0:T(8,128)(2,1)S(1)}, u32[]{:S(2)}, u32[]{:S(2)}) collective-permute-start(bf16[160,640]{1,0:T(8,128)(2,1)S(1)} %copy-done), channel_id=1, source_target_pairs={{8,0},{16,8},{24,16},{28,24},{20,28},{12,20},{4,12},{0,4},{9,1},{1... | collective-permute-start | bytes 614408 | tf_op jit(solution)/shard_map/ppermute | solution.py:342
  11.1 8.8 %collective-permute-start.1 = (bf16[160,640]{1,0:T(8,128)(2,1)S(1)}, bf16[160,640]{1,0:T(8,128)(2,1)S(1)}, u32[]{:S(2)}, u32[]{:S(2)}) collective-permute-start(bf16[160,640]{1,0:T(8,128)(2,1)S(1)} %collective-permute-done.refs_1_), channel_id=1, source_target_pairs={{0,8},{8,16},{16,24},{24,28},{28,20},{20,12},{12,4},{4,0},{1,9},{9... | collective-permute-start | bytes 614408 | tf_op jit(solution)/shard_map/ppermute | solution.py:339
  13.2 8.8 %collective-permute-start.11 = (bf16[160,640]{1,0:T(8,128)(2,1)S(1)}, bf16[160,640]{1,0:T(8,128)(2,1)S(1)}, u32[]{:S(2)}, u32[]{:S(2)}) collective-permute-start(bf16[160,640]{1,0:T(8,128)(2,1)S(1)} %collective-permute-done.10.refs_4_), channel_id=1, source_target_pairs={{8,0},{16,8},{24,16},{28,24},{20,28},{12,20},{4,12},{0,4},{9,1},{1... | collective-permute-start | bytes 614408 | tf_op jit(solution)/shard_map/ppermute | solution.py:340
  15.5 8.8 %collective-permute-start.8 = (bf16[160,640]{1,0:T(8,128)(2,1)S(1)}, bf16[160,640]{1,0:T(8,128)(2,1)S(1)}, u32[]{:S(2)}, u32[]{:S(2)}) collective-permute-start(bf16[160,640]{1,0:T(8,128)(2,1)S(1)} %collective-permute-done.7.refs_3_), channel_id=1, source_target_pairs={{0,8},{8,16},{16,24},{24,28},{28,20},{20,12},{12,4},{4,0},{1,9},{9... | collective-permute-start | bytes 614408 | tf_op jit(solution)/shard_map/ppermute | solution.py:341
  17.5 8.8 %collective-permute-start.5 = (bf16[160,640]{1,0:T(8,128)(2,1)S(1)}, bf16[160,640]{1,0:T(8,128)(2,1)S(1)}, u32[]{:S(2)}, u32[]{:S(2)}) collective-permute-start(bf16[160,640]{1,0:T(8,128)(2,1)S(1)} %collective-permute-done.4.refs_2_), channel_id=1, source_target_pairs={{8,0},{16,8},{24,16},{28,24},{20,28},{12,20},{4,12},{0,4},{9,1},{1... | collective-permute-start | bytes 614408 | tf_op jit(solution)/shard_map/ppermute | solution.py:342
  19.9 8.8 %collective-permute-start.2 = (bf16[160,640]{1,0:T(8,128)(2,1)S(1)}, bf16[160,640]{1,0:T(8,128)(2,1)S(1)}, u32[]{:S(2)}, u32[]{:S(2)}) collective-permute-start(bf16[160,640]{1,0:T(8,128)(2,1)S(1)} %collective-permute-done.1.refs_1_), channel_id=1, source_target_pairs={{0,8},{8,16},{16,24},{24,28},{28,20},{20,12},{12,4},{4,0},{1,9},{9... | collective-permute-start | bytes 614408 | tf_op jit(solution)/shard_map/ppermute | solution.py:339
  21.9 8.8 %collective-permute-start.12 = (bf16[160,640]{1,0:T(8,128)(2,1)S(1)}, bf16[160,640]{1,0:T(8,128)(2,1)S(1)}, u32[]{:S(2)}, u32[]{:S(2)}) collective-permute-start(bf16[160,640]{1,0:T(8,128)(2,1)S(1)} %collective-permute-done.11.refs_4_), channel_id=1, source_target_pairs={{8,0},{16,8},{24,16},{28,24},{20,28},{12,20},{4,12},{0,4},{9,1},{1... | collective-permute-start | bytes 614408 | tf_op jit(solution)/shard_map/ppermute | solution.py:340
  24.2 8.8 %collective-permute-start.9 = (bf16[160,640]{1,0:T(8,128)(2,1)S(1)}, bf16[160,640]{1,0:T(8,128)(2,1)S(1)}, u32[]{:S(2)}, u32[]{:S(2)}) collective-permute-start(bf16[160,640]{1,0:T(8,128)(2,1)S(1)} %collective-permute-done.8.refs_3_), channel_id=1, source_target_pairs={{0,8},{8,16},{16,24},{24,28},{28,20},{20,12},{12,4},{4,0},{1,9},{9... | collective-permute-start | bytes 614408 | tf_op jit(solution)/shard_map/ppermute | solution.py:341
  26.3 12.1 %collective-permute-start.6 = (bf16[160,640]{1,0:T(8,128)(2,1)S(1)}, bf16[160,640]{1,0:T(8,128)(2,1)S(1)}, u32[]{:S(2)}, u32[]{:S(2)}) collective-permute-start(bf16[160,640]{1,0:T(8,128)(2,1)S(1)} %collective-permute-done.5.refs_2_), channel_id=1, source_target_pairs={{8,0},{16,8},{24,16},{28,24},{20,28},{12,20},{4,12},{0,4},{9,1},{1... | collective-permute-start | bytes 614408 | tf_op jit(solution)/shard_map/ppermute | solution.py:342
  28.6 10.6 %collective-permute-start.3 = (bf16[160,640]{1,0:T(8,128)(2,1)S(1)}, bf16[160,640]{1,0:T(8,128)(2,1)S(1)}, u32[]{:S(2)}, u32[]{:S(2)}) collective-permute-start(bf16[160,640]{1,0:T(8,128)(2,1)S(1)} %collective-permute-done.2.refs_1_), channel_id=1, source_target_pairs={{0,8},{8,16},{16,24},{24,28},{28,20},{20,12},{12,4},{4,0},{1,9},{9... | collective-permute-start | bytes 614408 | tf_op jit(solution)/shard_map/ppermute | solution.py:344
  30.7 9.1 %collective-permute-start.13 = (bf16[128,640]{1,0:T(8,128)(2,1)S(1)}, bf16[128,640]{1,0:T(8,128)(2,1)S(1)}, u32[]{:S(2)}, u32[]{:S(2)}) collective-permute-start(bf16[128,640]{1,0:T(8,128)(2,1)S(1)} %slice.8), channel_id=1, source_target_pairs={{8,0},{16,8},{24,16},{28,24},{20,28},{12,20},{4,12},{0,4},{9,1},{1... | collective-permute-start | bytes 491528 | tf_op jit(solution)/shard_map/ppermute | solution.py:346
  33.0 6.8 %collective-permute-start.14 = (bf16[32,640]{1,0:T(8,128)(2,1)S(1)}, bf16[32,640]{1,0:T(8,128)(2,1)S(1)}, u32[]{:S(2)}, u32[]{:S(2)}) collective-permute-start(bf16[32,640]{1,0:T(8,128)(2,1)S(1)} %slice.9), channel_id=1, source_target_pairs={{0,8},{8,16},{16,24},{24,28},{28,20},{20,12},{12,4},{4,0},{1,9},{9... | collective-permute-start | bytes 122888 | tf_op jit(solution)/shard_map/ppermute | solution.py:347
  40.1 2.6 %collective-permute-start.15 = (bf16[160,640]{1,0:T(8,128)(2,1)S(1)}, bf16[160,640]{1,0:T(8,128)(2,1)S(1)}, u32[]{:S(2)}, u32[]{:S(2)}) collective-permute-start(bf16[160,640]{1,0:T(8,128)(2,1)S(1)} %last_values.1.a_ref), channel_id=1, source_target_pairs={{0,1},{1,0},{2,3},{3,2},{4,5},{5,4},{6,7},{7,6},{8,9},{9,8},{10,11... | collective-permute-start | bytes 614408 | tf_op jit(solution)/shard_map/ppermute | solution.py:350
  43.0 12.6 %collective-permute-start.18 = (bf16[160,512]{1,0:T(8,128)(2,1)S(1)}, bf16[160,512]{1,0:T(8,128)(2,1)S(1)}, u32[]{:S(2)}, u32[]{:S(2)}) collective-permute-start(bf16[160,512]{1,0:T(8,128)(2,1)S(1)} %project.10), channel_id=1, source_target_pairs={{0,2},{1,3},{2,0},{3,1},{4,6},{5,7},{6,4},{7,5},{8,10},{9,11},{10,... | collective-permute-start | bytes 491528 | tf_op jit(solution)/shard_map/ppermute | solution.py:360
  44.9 11.4 %collective-permute-start.17 = (bf16[160,512]{1,0:T(8,128)(2,1)S(1)}, bf16[160,512]{1,0:T(8,128)(2,1)S(1)}, u32[]{:S(2)}, u32[]{:S(2)}) collective-permute-start(bf16[160,512]{1,0:T(8,128)(2,1)S(1)} %project.9), channel_id=1, source_target_pairs={{0,2},{1,3},{2,0},{3,1},{4,6},{5,7},{6,4},{7,5},{8,10},{9,11},{10,... | collective-permute-start | bytes 491528 | tf_op jit(solution)/shard_map/ppermute | solution.py:360
  45.7 9.2 %collective-permute-start.19 = (bf16[160,256]{1,0:T(8,128)(2,1)S(1)}, bf16[160,256]{1,0:T(8,128)(2,1)S(1)}, u32[]{:S(2)}, u32[]{:S(2)}) collective-permute-start(bf16[160,256]{1,0:T(8,128)(2,1)S(1)} %project.11), channel_id=1, source_target_pairs={{0,2},{1,3},{2,0},{3,1},{4,6},{5,7},{6,4},{7,5},{8,10},{9,11},{10,... | collective-permute-start | bytes 245768 | tf_op jit(solution)/shard_map/ppermute | solution.py:360

commit v4 on v3

--- a/solution.py
+++ b/solution.py
@@ -181,7 +181,7 @@
             transcendentals=rows * count * heads,
             bytes_accessed=24 * rows * width,
         ),
-        compiler_params=params(),
+        compiler_params=pltpu.CompilerParams(vmem_limit_bytes=GRANT),
         name="last_scores",
     )(query, keys, *state)
 
@@ -245,6 +245,39 @@
     )(pltpu.with_memory_space_constraint(weight, pltpu.HBM))
 
 
+def far_kernel(chips, columns, w_ref, *refs):
+    place = lax.axis_index("head")
+    outs, sems = refs[:-1], refs[-1]
+    copies = []
+    for i, out in enumerate(outs):
+        target = lax.rem(place // 2 + i // 2 + 1, chips)
+        core = place % 2 if i % 2 == 0 else 1 - place % 2
+        start = pl.multiple_of((2 * target + core) * columns, HD)
+        copies.append(
+            pltpu.make_async_copy(w_ref.at[:, pl.ds(start, out.shape[1])], out, sems.at[i])
+        )
+        copies[-1].start()
+    for copy in copies:
+        copy.wait()
+
+
+def far_columns(weight, chips, columns, far):
+    depth = weight.shape[0]
+    many = 2 * (chips - 1)
+    return pl.pallas_call(
+        functools.partial(far_kernel, chips, columns),
+        out_shape=[jax.ShapeDtypeStruct((depth, far), weight.dtype)] * many,
+        in_specs=[HBM],
+        out_specs=[VM] * many,
+        scratch_shapes=[pltpu.SemaphoreType.DMA((many,))],
+        cost_estimate=pl.CostEstimate(
+            flops=0, transcendentals=0, bytes_accessed=4 * depth * far * many
+        ),
+        compiler_params=params(),
+        name="far_columns",
+    )(pltpu.with_memory_space_constraint(weight, pltpu.HBM))
+
+
 def project_kernel(first, tile, skip, a_ref, w_ref, *refs):
     out_ref = refs[-1]
     for start in range(0, out_ref.shape[1], tile):
@@ -285,7 +318,7 @@
     refs[-1][...] = total.astype(refs[-1].dtype)
 
 
-def finish(mine, parts, start, columns, output):
+def finish(mine, parts, start, columns, width, output):
     rows = mine.shape[0]
     args = (mine, *parts)
     specs = [VM] * len(args)
@@ -296,7 +329,7 @@
         specs.append(pl.BlockSpec(memory_space=pl.ANY))
     return pl.pallas_call(
         functools.partial(finish_kernel, start, len(parts)),
-        out_shape=jax.ShapeDtypeStruct(mine.shape, jnp.bfloat16),
+        out_shape=jax.ShapeDtypeStruct((rows, width), jnp.bfloat16),
         grid=(1,),
         in_specs=specs,
         out_specs=pl.BlockSpec((rows, columns), lambda i: (0, start // columns)),
@@ -309,9 +342,14 @@
     )(*args)
 
 
+def far_width(columns):
+    return columns * 2 // 5 // HD * HD
+
+
 def column_pieces(columns):
-    narrow = columns % PIECE or PIECE
-    return [(columns - narrow, narrow)] + [(c, PIECE) for c in range(0, columns - narrow, PIECE)]
+    far = far_width(columns)
+    narrow = (columns - far) % PIECE or PIECE
+    return [(c, PIECE) for c in range(far, columns - narrow, PIECE)] + [(columns - narrow, narrow)]
 
 
 def ring_pairs(n):
@@ -329,6 +367,15 @@
     pieces = column_pieces(columns)
     steps = n_seq // 2
 
+    hops = range(1, chips)
+    far = far_width(columns)
+    far_pairs = [[(i, (i + 2 * hop) % n_head) for i in range(n_head)] for hop in hops]
+    w_far = far_columns(out_weight, chips, columns, far)
+    w_same = [lax.ppermute(w_far[2 * h - 2], "head", far_pairs[h - 1]) for h in hops]
+    w_cross = [
+        lax.ppermute(w_far[2 * h - 1], "head", [(a, b ^ 1) for a, b in far_pairs[h - 1]])
+        for h in hops
+    ]
     w_give = weight_columns(out_weight, chips, columns, True)
     w_mine = weight_columns(out_weight, chips, columns, False)
     w_partner = lax.ppermute(w_give, "head", swap)
@@ -347,6 +394,7 @@
     v_lower = lax.ppermute(vf[upper:], "seq", ahead)
     expo, acc, norm = last_scores(queries, kf, state)
     attended = last_values(expo, v_upper, v_lower, acc, norm)
+    a_same = [lax.ppermute(attended, "head", far_pairs[h - 1]) for h in hops]
     partner = lax.ppermute(attended, "head", swap)
 
     away = (chips - 1) * columns
@@ -360,9 +408,14 @@
             arrived[index].append(lax.ppermute(given, "head", pairs))
     total = project(attended, w_mine, away, columns, None, 0, jnp.float32)
     total = project(partner, w_partner, away, columns, total, 0, jnp.float32)
-    output = None
+    a_cross = [lax.ppermute(a_same[h - 1], "head", swap) for h in hops]
+    near = total
+    for h in hops:
+        for far_rows, weight in ((a_same, w_same), (a_cross, w_cross)):
+            near = project(far_rows[h - 1], weight[h - 1], 0, far, near, 0, jnp.float32)
+    output = finish(near, [], 0, far, columns, None)
     for index, (start, piece) in enumerate(pieces):
-        output = finish(total, arrived[index], start, piece, output)
+        output = finish(total, arrived[index], start, piece, columns, output)
     return output
 
 

time: 57.1 us -> 74.8 us (1.31)
  waiting for transfers between devices: 21.9 us -> 35.5 us
  starting transfers between devices: 21.6 us -> 24 us
  Pallas kernels: 13.3 us -> 14.8 us
    ppermute x0 -> x4, waiting for transfers between devices: none -> 17.2 us  [the longest x1 17.2 us: on_device(): a_same = [lax.ppermute(attended, 'head', far_pairs[h - 1]) for h in hops]]
    ppermute x3, waiting for transfers between devices: 0.01 us -> 10.2 us  [on_device(): vb = lax.ppermute(vb, 'seq', back)]
    ppermute x3, waiting for transfers between devices: 6.8 us -> 0.01 us  [on_device(): vf = lax.ppermute(vf, 'seq', ahead)]
    ppermute x3 -> x2, waiting for transfers between devices: 6.66 us -> 3.01 us  [on_device(): arrived[index].append(lax.ppermute(given, 'head', pairs))]
    ppermute x0 -> x4, starting transfers between devices: none -> 3.52 us  [the longest x1 1.57 us: on_device(): a_same = [lax.ppermute(attended, 'head', far_pairs[h - 1]) for h in hops]]
    ppermute x4, waiting for transfers between devices: 8.41 us -> 5.01 us  [on_device(): kf = lax.ppermute(kf, 'seq', ahead)]
    ppermute x3, starting transfers between devices: 6.17 us -> 4.11 us  [on_device(): vf = lax.ppermute(vf, 'seq', ahead)]
    ppermute x3, starting transfers between devices: 0.04 us -> 1.98 us  [on_device(): vb = lax.ppermute(vb, 'seq', back)]
  transfers between devices with their start and end apart: 20 -> 23, of which waited for: 7 -> 9; matrix products, arithmetic and copies ran while one was open for 0% -> 0% of each run, Pallas kernels for 18% -> 16%
where the time goes in v4:
time: 74.8 us; the launch traced here: 74.6 us
  waiting for transfers between devices  35.5 us (47%)
  starting transfers between devices  24 us (32%)
  Pallas kernels  14.8 us (20%)
    ppermute x1, waiting for transfers between devices, on_device(): a_same = [lax.ppermute(attended, 'head', far_pairs[h - 1]) for h in hops]  17.2 us
    ppermute x3, waiting for transfers between devices, on_device(): vb = lax.ppermute(vb, 'seq', back)  10.2 us
    ppermute x4, starting transfers between devices, on_device(): kf = lax.ppermute(kf, 'seq', ahead)  8.37 us
    ppermute x4, waiting for transfers between devices, on_device(): kf = lax.ppermute(kf, 'seq', ahead)  5.01 us
    ppermute x3, starting transfers between devices, on_device(): vf = lax.ppermute(vf, 'seq', ahead)  4.11 us
    pallas_call x2, Pallas kernels, weight_columns(): pl.pallas_call(functools.partial(columns_kernel, chips, columns, partner)...  3.94 us
    ppermute x2, waiting for transfers between devices, on_device(): arrived[index].append(lax.ppermute(given, 'head', pairs))  3.01 us
    pallas_call x7, Pallas kernels, project(): pl.pallas_call(functools.partial(project_kernel, first, tile, skip), out_...  2.59 us
  transfers between devices with their start and end apart: 23, of which 9 were waited for; matrix products, arithmetic and copies ran while one was open for 0% of the time, Pallas kernels for 16%

profile of v4, /device:TPU:0, one launch (start us, length us, event | category | flops | bytes accessed | tf_op | source)
XLA Modules:
  0.0 74.6 jit_solution(10850006744264395168)
XLA Ops:
  0.0 2.0 %weight_columns.2 = bf16[640,2560]{1,0:T(8,128)(2,1)S(1)} custom-call(bf16[640,5120]{1,0:T(8,128)(2,1)} %w_ref.5), custom_call_target="tpu_custom_call" | custom-call | bytes 6553600 | tf_op jit(solution)/shard_map/weight_columns/pallas_call | solution.py:234
  2.0 0.6 collective-permute-start.16
  2.6 2.6 %collective-permute-start = (bf16[160,640]{1,0:T(8,128)(2,1)S(1)}, bf16[160,640]{1,0:T(8,128)(2,1)S(1)}, u32[]{:S(2)}, u32[]{:S(2)}) collective-permute-start(bf16[160,640]{1,0:T(8,128)(2,1)S(1)} %copy-done), channel_id=1, source_target_pairs={{0,8},{8,16},{16,24},{24,28},{28,20},{20,12},{12,4},{4,0},{1,9},{9... | collective-permute-start | bytes 614408 | tf_op jit(solution)/shard_map/ppermute | solution.py:386
  5.2 2.0 %collective-permute-start.10 = (bf16[160,640]{1,0:T(8,128)(2,1)S(1)}, bf16[160,640]{1,0:T(8,128)(2,1)S(1)}, u32[]{:S(2)}, u32[]{:S(2)}) collective-permute-start(bf16[160,640]{1,0:T(8,128)(2,1)S(1)} %copy-done.1), channel_id=1, source_target_pairs={{8,0},{16,8},{24,16},{28,24},{20,28},{12,20},{4,12},{0,4},{9,1},{1... | collective-permute-start | bytes 614408 | tf_op jit(solution)/shard_map/ppermute | solution.py:387
  7.3 3.8 %collective-permute-done.refs_1_ = bf16[160,640]{1,0:T(8,128)(2,1)S(1)} collective-permute-done((bf16[160,640]{1,0:T(8,128)(2,1)S(1)}, bf16[160,640]{1,0:T(8,128)(2,1)S(1)}, u32[]{:S(2)}, u32[]{:S(2)}) %collective-permute-start) | collective-permute-done | bytes 204832 | tf_op jit(solution)/shard_map/ppermute | solution.py:386
  11.1 2.1 %collective-permute-start.1 = (bf16[160,640]{1,0:T(8,128)(2,1)S(1)}, bf16[160,640]{1,0:T(8,128)(2,1)S(1)}, u32[]{:S(2)}, u32[]{:S(2)}) collective-permute-start(bf16[160,640]{1,0:T(8,128)(2,1)S(1)} %collective-permute-done.refs_1_), channel_id=1, source_target_pairs={{0,8},{8,16},{16,24},{24,28},{28,20},{20,12},{12,4},{4,0},{1,9},{9... | collective-permute-start | bytes 614408 | tf_op jit(solution)/shard_map/ppermute | solution.py:386
  13.2 4.4 %collective-permute-done.10.refs_4_ = bf16[160,640]{1,0:T(8,128)(2,1)S(1)} collective-permute-done((bf16[160,640]{1,0:T(8,128)(2,1)S(1)}, bf16[160,640]{1,0:T(8,128)(2,1)S(1)}, u32[]{:S(2)}, u32[]{:S(2)}) %collective-permute-start.10) | collective-permute-done | bytes 204832 | tf_op jit(solution)/shard_map/ppermute | solution.py:387
  17.6 2.0 %collective-permute-start.8 = (bf16[160,640]{1,0:T(8,128)(2,1)S(1)}, bf16[160,640]{1,0:T(8,128)(2,1)S(1)}, u32[]{:S(2)}, u32[]{:S(2)}) collective-permute-start(bf16[160,640]{1,0:T(8,128)(2,1)S(1)} %collective-permute-done.7.refs_3_), channel_id=1, source_target_pairs={{0,8},{8,16},{16,24},{24,28},{28,20},{20,12},{12,4},{4,0},{1,9},{9... | collective-permute-start | bytes 614408 | tf_op jit(solution)/shard_map/ppermute | solution.py:388
  19.9 2.1 %collective-permute-start.2 = (bf16[160,640]{1,0:T(8,128)(2,1)S(1)}, bf16[160,640]{1,0:T(8,128)(2,1)S(1)}, u32[]{:S(2)}, u32[]{:S(2)}) collective-permute-start(bf16[160,640]{1,0:T(8,128)(2,1)S(1)} %collective-permute-done.1.refs_1_), channel_id=1, source_target_pairs={{0,8},{8,16},{16,24},{24,28},{28,20},{20,12},{12,4},{4,0},{1,9},{9... | collective-permute-start | bytes 614408 | tf_op jit(solution)/shard_map/ppermute | solution.py:386
  21.9 4.4 %collective-permute-done.11.refs_4_ = bf16[160,640]{1,0:T(8,128)(2,1)S(1)} collective-permute-done((bf16[160,640]{1,0:T(8,128)(2,1)S(1)}, bf16[160,640]{1,0:T(8,128)(2,1)S(1)}, u32[]{:S(2)}, u32[]{:S(2)}) %collective-permute-start.11) | collective-permute-done | bytes 204832 | tf_op jit(solution)/shard_map/ppermute | solution.py:387
  26.3 2.0 %collective-permute-start.9 = (bf16[160,640]{1,0:T(8,128)(2,1)S(1)}, bf16[160,640]{1,0:T(8,128)(2,1)S(1)}, u32[]{:S(2)}, u32[]{:S(2)}) collective-permute-start(bf16[160,640]{1,0:T(8,128)(2,1)S(1)} %collective-permute-done.8.refs_3_), channel_id=1, source_target_pairs={{0,8},{8,16},{16,24},{24,28},{28,20},{20,12},{12,4},{4,0},{1,9},{9... | collective-permute-start | bytes 614408 | tf_op jit(solution)/shard_map/ppermute | solution.py:388
  28.4 1.3 %far_columns.1 = (bf16[640,512]{1,0:T(8,128)(2,1)S(1)}, bf16[640,512]{1,0:T(8,128)(2,1)S(1)}) custom-call(bf16[640,5120]{1,0:T(8,128)(2,1)} %w_ref.5), custom_call_target="tpu_custom_call" | custom-call | bytes 2621440 | tf_op jit(solution)/shard_map/far_columns/pallas_call | solution.py:267
  29.7 1.6 %collective-permute-start.22 = (bf16[640,512]{1,0:T(8,128)(2,1)S(1)}, bf16[640,512]{1,0:T(8,128)(2,1)S(1)}, u32[]{:S(2)}, u32[]{:S(2)}) collective-permute-start(bf16[640,512]{1,0:T(8,128)(2,1)S(1)} %get-tuple-element.40), channel_id=1, source_target_pairs={{0,2},{1,3},{2,0},{3,1},{4,6},{5,7},{6,4},{7,5},{8,10},{9,11},{10,... | collective-permute-start | bytes 1966088 | tf_op jit(solution)/shard_map/ppermute | solution.py:374
  31.2 1.6 %collective-permute-start.3 = (bf16[160,640]{1,0:T(8,128)(2,1)S(1)}, bf16[160,640]{1,0:T(8,128)(2,1)S(1)}, u32[]{:S(2)}, u32[]{:S(2)}) collective-permute-start(bf16[160,640]{1,0:T(8,128)(2,1)S(1)} %collective-permute-done.2.refs_1_), channel_id=1, source_target_pairs={{0,8},{8,16},{16,24},{24,28},{28,20},{20,12},{12,4},{4,0},{1,9},{9... | collective-permute-start | bytes 614408 | tf_op jit(solution)/shard_map/ppermute | solution.py:391
  32.8 1.5 %collective-permute-done.12.refs_4_ = bf16[160,640]{1,0:T(8,128)(2,1)S(1)} collective-permute-done((bf16[160,640]{1,0:T(8,128)(2,1)S(1)}, bf16[160,640]{1,0:T(8,128)(2,1)S(1)}, u32[]{:S(2)}, u32[]{:S(2)}) %collective-permute-start.12) | collective-permute-done | bytes 204832 | tf_op jit(solution)/shard_map/ppermute | solution.py:387
  34.7 1.5 %collective-permute-start.13 = (bf16[128,640]{1,0:T(8,128)(2,1)S(1)}, bf16[128,640]{1,0:T(8,128)(2,1)S(1)}, u32[]{:S(2)}, u32[]{:S(2)}) collective-permute-start(bf16[128,640]{1,0:T(8,128)(2,1)S(1)} %slice.8), channel_id=1, source_target_pairs={{8,0},{16,8},{24,16},{28,24},{20,28},{12,20},{4,12},{0,4},{9,1},{1... | collective-permute-start | bytes 491528 | tf_op jit(solution)/shard_map/ppermute | solution.py:393
  36.2 0.9 %collective-permute-done.3.k_ref = bf16[160,640]{1,0:T(8,128)(2,1)S(1)} collective-permute-done((bf16[160,640]{1,0:T(8,128)(2,1)S(1)}, bf16[160,640]{1,0:T(8,128)(2,1)S(1)}, u32[]{:S(2)}, u32[]{:S(2)}) %collective-permute-start.3) | collective-permute-done | bytes 204832 | tf_op jit(solution)/shard_map/ppermute | solution.py:391
  37.2 1.8 %collective-permute-start.14 = (bf16[32,640]{1,0:T(8,128)(2,1)S(1)}, bf16[32,640]{1,0:T(8,128)(2,1)S(1)}, u32[]{:S(2)}, u32[]{:S(2)}) collective-permute-start(bf16[32,640]{1,0:T(8,128)(2,1)S(1)} %slice.9), channel_id=1, source_target_pairs={{0,8},{8,16},{16,24},{24,28},{28,20},{20,12},{12,4},{4,0},{1,9},{9... | collective-permute-start | bytes 122888 | tf_op jit(solution)/shard_map/ppermute | solution.py:394
  39.0 1.7 %first_flash.1 = (f32[160,640]{1,0:T(8,128)S(1)}, f32[160,640]{1,0:T(8,128)S(1)}, f32[160,640]{1,0:T(8,128)S(1)}, bf16[160,640]{1,0:T(8,128)(2,1)S(1)}) custom-call(bf16[160,640]{1,0:T(8,128)(2,1)} %q_hbm.1, bf16[160,640]{1,0:T(8,128)(2,1)} %k_hbm.1, bf16[160,640]{1,0:T(8,128)(2,1)} %v_hbm.1), custom_call_target="tpu_custom_call" | custom-call | flops 65536000 | bytes 2048000 | tf_op jit(solution)/shard_map/first_flash/pallas_call | solution.py:125
  40.7 0.8 %flash.3 = (f32[160,640]{1,0:T(8,128)S(1)}, f32[160,640]{1,0:T(8,128)S(1)}, f32[160,640]{1,0:T(8,128)S(1)}) custom-call(bf16[160,640]{1,0:T(8,128)(2,1)S(1)} %get-tuple-element.23.refs_0_.q_ref, bf16[160,640]{1,0:T(8,128)(2,1)S(1)} %collective-permute-done.refs_1_, bf16[160,640]{1,0:T(8,128)(2,1)S(1)} %collective-permute-done.4.refs_2_, ...), custom_call_target="tpu_custom_call" | custom-call | flops 131072000 | bytes 3481600 | tf_op jit(solution)/shard_map/flash/pallas_call | solution.py:95
  41.5 0.8 %flash.4 = (f32[160,640]{1,0:T(8,128)S(1)}, f32[160,640]{1,0:T(8,128)S(1)}, f32[160,640]{1,0:T(8,128)S(1)}) custom-call(bf16[160,640]{1,0:T(8,128)(2,1)S(1)} %get-tuple-element.23.refs_0_.q_ref, bf16[160,640]{1,0:T(8,128)(2,1)S(1)} %collective-permute-done.1.refs_1_, bf16[160,640]{1,0:T(8,128)(2,1)S(1)} %collective-permute-done.5.refs_2_, ...), custom_call_target="tpu_custom_call" | custom-call | flops 131072000 | bytes 3481600 | tf_op jit(solution)/shard_map/flash/pallas_call | solution.py:95
  42.3 0.8 %flash.5 = (f32[160,640]{1,0:T(8,128)S(1)}, f32[160,640]{1,0:T(8,128)S(1)}, f32[160,640]{1,0:T(8,128)S(1)}) custom-call(bf16[160,640]{1,0:T(8,128)(2,1)S(1)} %get-tuple-element.23.refs_0_.q_ref, bf16[160,640]{1,0:T(8,128)(2,1)S(1)} %collective-permute-done.2.refs_1_, bf16[160,640]{1,0:T(8,128)(2,1)S(1)} %collective-permute-done.6.refs_2_, ...), custom_call_target="tpu_custom_call" | custom-call | flops 131072000 | bytes 3481600 | tf_op jit(solution)/shard_map/flash/pallas_call | solution.py:95
  43.9 1.6 %collective-permute-start.19 = (bf16[160,640]{1,0:T(8,128)(2,1)S(1)}, bf16[160,640]{1,0:T(8,128)(2,1)S(1)}, u32[]{:S(2)}, u32[]{:S(2)}) collective-permute-start(bf16[160,640]{1,0:T(8,128)(2,1)S(1)} %last_values.1.a_ref), channel_id=1, source_target_pairs={{0,2},{1,3},{2,0},{3,1},{4,6},{5,7},{6,4},{7,5},{8,10},{9,11},{10,... | collective-permute-start | bytes 614408 | tf_op jit(solution)/shard_map/ppermute | solution.py:397
  45.5 17.2 %collective-permute-done.19.a_ref = bf16[160,640]{1,0:T(8,128)(2,1)S(1)} collective-permute-done((bf16[160,640]{1,0:T(8,128)(2,1)S(1)}, bf16[160,640]{1,0:T(8,128)(2,1)S(1)}, u32[]{:S(2)}, u32[]{:S(2)}) %collective-permute-start.19) | collective-permute-done | bytes 204832 | tf_op jit(solution)/shard_map/ppermute | solution.py:397
  62.7 1.9 %weight_columns.3.w_ref = bf16[640,2560]{1,0:T(8,128)(2,1)S(1)} custom-call(bf16[640,5120]{1,0:T(8,128)(2,1)} %w_ref.5), custom_call_target="tpu_custom_call" | custom-call | bytes 6553600 | tf_op jit(solution)/shard_map/weight_columns/pallas_call | solution.py:234
  65.5 1.6 %collective-permute-start.18 = (bf16[160,512]{1,0:T(8,128)(2,1)S(1)}, bf16[160,512]{1,0:T(8,128)(2,1)S(1)}, u32[]{:S(2)}, u32[]{:S(2)}) collective-permute-start(bf16[160,512]{1,0:T(8,128)(2,1)S(1)} %project.11), channel_id=1, source_target_pairs={{0,2},{1,3},{2,0},{3,1},{4,6},{5,7},{6,4},{7,5},{8,10},{9,11},{10,... | collective-permute-start | bytes 491528 | tf_op jit(solution)/shard_map/ppermute | solution.py:408
  67.3 0.6 collective-permute-start.17
  69.5 0.7 finish.3.refs_2_
  70.2 2.4 %collective-permute-done.18.refs_1_ = bf16[160,512]{1,0:T(8,128)(2,1)S(1)} collective-permute-done((bf16[160,512]{1,0:T(8,128)(2,1)S(1)}, bf16[160,512]{1,0:T(8,128)(2,1)S(1)}, u32[]{:S(2)}, u32[]{:S(2)}) %collective-permute-start.18) | collective-permute-done | bytes 163872 | tf_op jit(solution)/shard_map/ppermute | solution.py:408
  72.7 0.7 finish.4.refs_2_
  73.4 0.6 collective-permute-done.17.refs_1_
  73.9 0.7 finish.5
  (39 shorter events, 4.3 us)
Async XLA Ops:
  0.0 2.6 %copy-start = (bf16[160,640]{1,0:T(8,128)(2,1)S(1)}, bf16[160,640]{1,0:T(8,128)(2,1)}, u32[]{:S(2)}) copy-start(bf16[160,640]{1,0:T(8,128)(2,1)} %k_hbm.1) | copy-start | bytes 614404
  0.0 5.2 %copy-start.1 = (bf16[160,640]{1,0:T(8,128)(2,1)S(1)}, bf16[160,640]{1,0:T(8,128)(2,1)}, u32[]{:S(2)}) copy-start(bf16[160,640]{1,0:T(8,128)(2,1)} %v_hbm.1) | copy-start | bytes 614404
  2.0 63.2 %collective-permute-start.16 = (bf16[640,2560]{1,0:T(8,128)(2,1)S(1)}, bf16[640,2560]{1,0:T(8,128)(2,1)S(1)}, u32[]{:S(2)}, u32[]{:S(2)}) collective-permute-start(bf16[640,2560]{1,0:T(8,128)(2,1)S(1)} %weight_columns.2), channel_id=1, source_target_pairs={{0,1},{1,0},{2,3},{3,2},{4,5},{5,4},{6,7},{7,6},{8,9},{9,8},{10,11... | collective-permute-start | bytes 9830408 | tf_op jit(solution)/shard_map/ppermute | solution.py:381
  2.6 8.5 %collective-permute-start = (bf16[160,640]{1,0:T(8,128)(2,1)S(1)}, bf16[160,640]{1,0:T(8,128)(2,1)S(1)}, u32[]{:S(2)}, u32[]{:S(2)}) collective-permute-start(bf16[160,640]{1,0:T(8,128)(2,1)S(1)} %copy-done), channel_id=1, source_target_pairs={{0,8},{8,16},{16,24},{24,28},{28,20},{20,12},{12,4},{4,0},{1,9},{9... | collective-permute-start | bytes 614408 | tf_op jit(solution)/shard_map/ppermute | solution.py:386
  5.2 8.0 %collective-permute-start.4 = (bf16[160,640]{1,0:T(8,128)(2,1)S(1)}, bf16[160,640]{1,0:T(8,128)(2,1)S(1)}, u32[]{:S(2)}, u32[]{:S(2)}) collective-permute-start(bf16[160,640]{1,0:T(8,128)(2,1)S(1)} %copy-done), channel_id=1, source_target_pairs={{8,0},{16,8},{24,16},{28,24},{20,28},{12,20},{4,12},{0,4},{9,1},{1... | collective-permute-start | bytes 614408 | tf_op jit(solution)/shard_map/ppermute | solution.py:389
  5.2 12.3 %collective-permute-start.10 = (bf16[160,640]{1,0:T(8,128)(2,1)S(1)}, bf16[160,640]{1,0:T(8,128)(2,1)S(1)}, u32[]{:S(2)}, u32[]{:S(2)}) collective-permute-start(bf16[160,640]{1,0:T(8,128)(2,1)S(1)} %copy-done.1), channel_id=1, source_target_pairs={{8,0},{16,8},{24,16},{28,24},{20,28},{12,20},{4,12},{0,4},{9,1},{1... | collective-permute-start | bytes 614408 | tf_op jit(solution)/shard_map/ppermute | solution.py:387
  7.2 10.4 %collective-permute-start.7 = (bf16[160,640]{1,0:T(8,128)(2,1)S(1)}, bf16[160,640]{1,0:T(8,128)(2,1)S(1)}, u32[]{:S(2)}, u32[]{:S(2)}) collective-permute-start(bf16[160,640]{1,0:T(8,128)(2,1)S(1)} %copy-done.1), channel_id=1, source_target_pairs={{0,8},{8,16},{16,24},{24,28},{28,20},{20,12},{12,4},{4,0},{1,9},{9... | collective-permute-start | bytes 614408 | tf_op jit(solution)/shard_map/ppermute | solution.py:388
  11.1 8.8 %collective-permute-start.1 = (bf16[160,640]{1,0:T(8,128)(2,1)S(1)}, bf16[160,640]{1,0:T(8,128)(2,1)S(1)}, u32[]{:S(2)}, u32[]{:S(2)}) collective-permute-start(bf16[160,640]{1,0:T(8,128)(2,1)S(1)} %collective-permute-done.refs_1_), channel_id=1, source_target_pairs={{0,8},{8,16},{16,24},{24,28},{28,20},{20,12},{12,4},{4,0},{1,9},{9... | collective-permute-start | bytes 614408 | tf_op jit(solution)/shard_map/ppermute | solution.py:386
  13.2 8.8 %collective-permute-start.5 = (bf16[160,640]{1,0:T(8,128)(2,1)S(1)}, bf16[160,640]{1,0:T(8,128)(2,1)S(1)}, u32[]{:S(2)}, u32[]{:S(2)}) collective-permute-start(bf16[160,640]{1,0:T(8,128)(2,1)S(1)} %collective-permute-done.4.refs_2_), channel_id=1, source_target_pairs={{8,0},{16,8},{24,16},{28,24},{20,28},{12,20},{4,12},{0,4},{9,1},{1... | collective-permute-start | bytes 614408 | tf_op jit(solution)/shard_map/ppermute | solution.py:389
  17.5 8.8 %collective-permute-start.11 = (bf16[160,640]{1,0:T(8,128)(2,1)S(1)}, bf16[160,640]{1,0:T(8,128)(2,1)S(1)}, u32[]{:S(2)}, u32[]{:S(2)}) collective-permute-start(bf16[160,640]{1,0:T(8,128)(2,1)S(1)} %collective-permute-done.10.refs_4_), channel_id=1, source_target_pairs={{8,0},{16,8},{24,16},{28,24},{20,28},{12,20},{4,12},{0,4},{9,1},{1... | collective-permute-start | bytes 614408 | tf_op jit(solution)/shard_map/ppermute | solution.py:387
  17.6 8.8 %collective-permute-start.8 = (bf16[160,640]{1,0:T(8,128)(2,1)S(1)}, bf16[160,640]{1,0:T(8,128)(2,1)S(1)}, u32[]{:S(2)}, u32[]{:S(2)}) collective-permute-start(bf16[160,640]{1,0:T(8,128)(2,1)S(1)} %collective-permute-done.7.refs_3_), channel_id=1, source_target_pairs={{0,8},{8,16},{16,24},{24,28},{28,20},{20,12},{12,4},{4,0},{1,9},{9... | collective-permute-start | bytes 614408 | tf_op jit(solution)/shard_map/ppermute | solution.py:388
  19.9 9.8 %collective-permute-start.2 = (bf16[160,640]{1,0:T(8,128)(2,1)S(1)}, bf16[160,640]{1,0:T(8,128)(2,1)S(1)}, u32[]{:S(2)}, u32[]{:S(2)}) collective-permute-start(bf16[160,640]{1,0:T(8,128)(2,1)S(1)} %collective-permute-done.1.refs_1_), channel_id=1, source_target_pairs={{0,8},{8,16},{16,24},{24,28},{28,20},{20,12},{12,4},{4,0},{1,9},{9... | collective-permute-start | bytes 614408 | tf_op jit(solution)/shard_map/ppermute | solution.py:386
  21.9 9.3 %collective-permute-start.6 = (bf16[160,640]{1,0:T(8,128)(2,1)S(1)}, bf16[160,640]{1,0:T(8,128)(2,1)S(1)}, u32[]{:S(2)}, u32[]{:S(2)}) collective-permute-start(bf16[160,640]{1,0:T(8,128)(2,1)S(1)} %collective-permute-done.5.refs_2_), channel_id=1, source_target_pairs={{8,0},{16,8},{24,16},{28,24},{20,28},{12,20},{4,12},{0,4},{9,1},{1... | collective-permute-start | bytes 614408 | tf_op jit(solution)/shard_map/ppermute | solution.py:389
  26.3 8.0 %collective-permute-start.12 = (bf16[160,640]{1,0:T(8,128)(2,1)S(1)}, bf16[160,640]{1,0:T(8,128)(2,1)S(1)}, u32[]{:S(2)}, u32[]{:S(2)}) collective-permute-start(bf16[160,640]{1,0:T(8,128)(2,1)S(1)} %collective-permute-done.11.refs_4_), channel_id=1, source_target_pairs={{8,0},{16,8},{24,16},{28,24},{20,28},{12,20},{4,12},{0,4},{9,1},{1... | collective-permute-start | bytes 614408 | tf_op jit(solution)/shard_map/ppermute | solution.py:387
  26.3 8.4 %collective-permute-start.9 = (bf16[160,640]{1,0:T(8,128)(2,1)S(1)}, bf16[160,640]{1,0:T(8,128)(2,1)S(1)}, u32[]{:S(2)}, u32[]{:S(2)}) collective-permute-start(bf16[160,640]{1,0:T(8,128)(2,1)S(1)} %collective-permute-done.8.refs_3_), channel_id=1, source_target_pairs={{0,8},{8,16},{16,24},{24,28},{28,20},{20,12},{12,4},{4,0},{1,9},{9... | collective-permute-start | bytes 614408 | tf_op jit(solution)/shard_map/ppermute | solution.py:388
  29.7 39.2 %collective-permute-start.22 = (bf16[640,512]{1,0:T(8,128)(2,1)S(1)}, bf16[640,512]{1,0:T(8,128)(2,1)S(1)}, u32[]{:S(2)}, u32[]{:S(2)}) collective-permute-start(bf16[640,512]{1,0:T(8,128)(2,1)S(1)} %get-tuple-element.40), channel_id=1, source_target_pairs={{0,2},{1,3},{2,0},{3,1},{4,6},{5,7},{6,4},{7,5},{8,10},{9,11},{10,... | collective-permute-start | bytes 1966088 | tf_op jit(solution)/shard_map/ppermute | solution.py:374
  31.2 5.9 %collective-permute-start.3 = (bf16[160,640]{1,0:T(8,128)(2,1)S(1)}, bf16[160,640]{1,0:T(8,128)(2,1)S(1)}, u32[]{:S(2)}, u32[]{:S(2)}) collective-permute-start(bf16[160,640]{1,0:T(8,128)(2,1)S(1)} %collective-permute-done.2.refs_1_), channel_id=1, source_target_pairs={{0,8},{8,16},{16,24},{24,28},{28,20},{20,12},{12,4},{4,0},{1,9},{9... | collective-permute-start | bytes 614408 | tf_op jit(solution)/shard_map/ppermute | solution.py:391
  34.3 34.9 %collective-permute-start.21 = (bf16[640,512]{1,0:T(8,128)(2,1)S(1)}, bf16[640,512]{1,0:T(8,128)(2,1)S(1)}, u32[]{:S(2)}, u32[]{:S(2)}) collective-permute-start(bf16[640,512]{1,0:T(8,128)(2,1)S(1)} %get-tuple-element.39), channel_id=1, source_target_pairs={{0,3},{1,2},{2,1},{3,0},{4,7},{5,6},{6,5},{7,4},{8,11},{9,10},{10,... | collective-permute-start | bytes 1966088 | tf_op jit(solution)/shard_map/ppermute | solution.py:376
  34.7 9.0 %collective-permute-start.13 = (bf16[128,640]{1,0:T(8,128)(2,1)S(1)}, bf16[128,640]{1,0:T(8,128)(2,1)S(1)}, u32[]{:S(2)}, u32[]{:S(2)}) collective-permute-start(bf16[128,640]{1,0:T(8,128)(2,1)S(1)} %slice.8), channel_id=1, source_target_pairs={{8,0},{16,8},{24,16},{28,24},{20,28},{12,20},{4,12},{0,4},{9,1},{1... | collective-permute-start | bytes 491528 | tf_op jit(solution)/shard_map/ppermute | solution.py:393
  37.2 6.5 %collective-permute-start.14 = (bf16[32,640]{1,0:T(8,128)(2,1)S(1)}, bf16[32,640]{1,0:T(8,128)(2,1)S(1)}, u32[]{:S(2)}, u32[]{:S(2)}) collective-permute-start(bf16[32,640]{1,0:T(8,128)(2,1)S(1)} %slice.9), channel_id=1, source_target_pairs={{0,8},{8,16},{16,24},{24,28},{28,20},{20,12},{12,4},{4,0},{1,9},{9... | collective-permute-start | bytes 122888 | tf_op jit(solution)/shard_map/ppermute | solution.py:394
  43.9 18.8 %collective-permute-start.19 = (bf16[160,640]{1,0:T(8,128)(2,1)S(1)}, bf16[160,640]{1,0:T(8,128)(2,1)S(1)}, u32[]{:S(2)}, u32[]{:S(2)}) collective-permute-start(bf16[160,640]{1,0:T(8,128)(2,1)S(1)} %last_values.1.a_ref), channel_id=1, source_target_pairs={{0,2},{1,3},{2,0},{3,1},{4,6},{5,7},{6,4},{7,5},{8,10},{9,11},{10,... | collective-permute-start | bytes 614408 | tf_op jit(solution)/shard_map/ppermute | solution.py:397
  45.5 19.7 %collective-permute-start.15 = (bf16[160,640]{1,0:T(8,128)(2,1)S(1)}, bf16[160,640]{1,0:T(8,128)(2,1)S(1)}, u32[]{:S(2)}, u32[]{:S(2)}) collective-permute-start(bf16[160,640]{1,0:T(8,128)(2,1)S(1)} %last_values.1.a_ref), channel_id=1, source_target_pairs={{0,1},{1,0},{2,3},{3,2},{4,5},{5,4},{6,7},{7,6},{8,9},{9,8},{10,11... | collective-permute-start | bytes 614408 | tf_op jit(solution)/shard_map/ppermute | solution.py:398
  62.7 6.5 %collective-permute-start.20 = (bf16[160,640]{1,0:T(8,128)(2,1)S(1)}, bf16[160,640]{1,0:T(8,128)(2,1)S(1)}, u32[]{:S(2)}, u32[]{:S(2)}) collective-permute-start(bf16[160,640]{1,0:T(8,128)(2,1)S(1)} %collective-permute-done.19.a_ref), channel_id=1, source_target_pairs={{0,1},{1,0},{2,3},{3,2},{4,5},{5,4},{6,7},{7,6},{8,9},{9,8},{10,11... | collective-permute-start | bytes 614408 | tf_op jit(solution)/shard_map/ppermute | solution.py:411
  65.5 7.1 %collective-permute-start.18 = (bf16[160,512]{1,0:T(8,128)(2,1)S(1)}, bf16[160,512]{1,0:T(8,128)(2,1)S(1)}, u32[]{:S(2)}, u32[]{:S(2)}) collective-permute-start(bf16[160,512]{1,0:T(8,128)(2,1)S(1)} %project.11), channel_id=1, source_target_pairs={{0,2},{1,3},{2,0},{3,1},{4,6},{5,7},{6,4},{7,5},{8,10},{9,11},{10,... | collective-permute-start | bytes 491528 | tf_op jit(solution)/shard_map/ppermute | solution.py:408
  67.3 6.6 %collective-permute-start.17 = (bf16[160,256]{1,0:T(8,128)(2,1)S(1)}, bf16[160,256]{1,0:T(8,128)(2,1)S(1)}, u32[]{:S(2)}, u32[]{:S(2)}) collective-permute-start(bf16[160,256]{1,0:T(8,128)(2,1)S(1)} %project.10), channel_id=1, source_target_pairs={{0,2},{1,3},{2,0},{3,1},{4,6},{5,7},{6,4},{7,5},{8,10},{9,11},{10,... | collective-permute-start | bytes 245768 | tf_op jit(solution)/shard_map/ppermute | solution.py:408
